TPU v7x, 32 devices: a whole 2x2x4 slice. The times are simulated.
32 devices in a mesh: row: 8 (over z, x), col: 4 (over y, core).
Axes of the slice: x: 2, y: 2, z: 4, core: 2. Of those that a mesh axis runs over, the one named last changes fastest.
Arguments:
- inverse: float32 [12288, 12288], P('row', 'col'), may hold values from -0.21875 to 0.21875
- pattern: int32 [24, 24], replicated, may hold values from 0 to 1, as said below
- factor: float32 [12288, 1024], P(('row', 'col')), may hold values from -0.4375 to 0.4375
- diag_inverse: float32 [1024, 1024], replicated, may hold values from -6 to 6
Outputs:
- panel_out: float32 [12288, 1024], P(('row', 'col'))
- diag_block: float32 [1024, 1024], replicated
Inputs may be any that keep to these rules, and one draw needn't show every extreme that they name: pattern[i, j] is 1 where tile (i, j) of the inverse is stored, else 0.
All inputs are finite; a program needn't handle non-finite values.
Results may differ from a plain program's by a relative error of at most 0.000075.
Values sent between devices are 32-bit elements; how exact they have to be, the bound alone decides.
No kernel may reach another device: no remote copies, remote signals or barrier semaphores. Data moves between devices by JAX's collectives and lax.ppermute only.
A program may use at most 128 MiB of HBM per device.

v0:
```python
import jax
import jax.numpy as jnp
from jax import lax
from jax.sharding import PartitionSpec as P

B = 512
W = 1024


HIGHEST = lax.Precision.HIGHEST


def add_product(running, tile_row, inv_block, rows_part):
    first = tile_row * B
    current = lax.dynamic_slice_in_dim(running, first, B, 0)
    update = current + jnp.dot(inv_block, rows_part, precision=HIGHEST)
    return lax.dynamic_update_slice_in_dim(running, update, first, 0)


def stored_list(pattern, first_row, first_col, tile_rows, tile_cols):
    window = lax.dynamic_slice(pattern, (first_row, first_col), (tile_rows, tile_cols)).reshape(-1)
    count_all = tile_rows * tile_cols
    places = jnp.where(window > 0, jnp.cumsum(window) - 1, count_all)
    listing = (
        jnp.zeros((count_all + 1,), jnp.int32)
        .at[places]
        .set(jnp.arange(count_all, dtype=jnp.int32))
    )
    return (listing[:count_all], jnp.sum(window))


def body(inverse, pattern, factor, diag_inverse):
    row_count = lax.axis_size("row")
    col_count = lax.axis_size("col")
    group_ratio = row_count // col_count
    my_column = lax.axis_index("col")
    tile_rows = inverse.shape[0] // B
    tile_cols = inverse.shape[1] // B
    first_row = lax.axis_index("row") * tile_rows
    gathered = lax.all_gather(factor, "row", axis=0, tiled=True)
    arrived = lax.all_to_all(gathered, "col", split_axis=0, concat_axis=0, tiled=True)
    column_block = (
        arrived.reshape(col_count, group_ratio, factor.shape[0], W)
        .transpose(1, 0, 2, 3)
        .reshape(-1, W)
    )
    listing, mine_count = stored_list(
        pattern, first_row, my_column * tile_cols, tile_rows, tile_cols
    )

    def local_step(position, running):
        chosen = listing[position]
        tile_row = chosen // tile_cols
        tile_col = chosen % tile_cols
        inv_block = lax.dynamic_slice(inverse, (tile_row * B, tile_col * B), (B, B))
        rows_part = lax.dynamic_slice_in_dim(column_block, tile_col * B, B, 0)
        return add_product(running, tile_row, inv_block, rows_part)

    partial_sum = jnp.zeros((inverse.shape[0], W), jnp.float32)
    partial_sum = lax.fori_loop(0, mine_count, local_step, partial_sum)
    outer_local = None
    panel_sum = lax.psum_scatter(partial_sum, "col", scatter_dimension=0, tiled=True)
    outer_local = jnp.dot(factor.T, panel_sum, precision=HIGHEST)
    diag_block = diag_inverse + lax.psum(outer_local, ("row", "col"))
    return (-panel_sum, diag_block)


def solution(mesh):
    return jax.shard_map(
        body,
        mesh=mesh,
        in_specs=(P("row", "col"), P(), P(("row", "col"), None), P()),
        out_specs=(P(("row", "col"), None), P()),
        check_vma=False,
    )
```

profile of v0, /device:TPU:0, one launch (start us, length us, event | category | flops | bytes accessed | tf_op | source)
XLA Modules:
  0.0 767.1 jit_solution(14343638074206742556)
XLA Ops:
  7.2 0.0 all-gather.2.cloned.1.call-start
  7.2 0.7 all-gather.2.cloned.1.call-update
  7.9 181.1 %all-gather.2.cloned.1.call-done = f32[3072,1024]{1,0:T(8,128)} async-done(((f32[384,1024]{1,0:T(8,128)}), f32[3072,1024]{1,0:T(8,128)}) %all-gather.2.cloned.1.call-update) | async-done | bytes 12582928 | tf_op jit(solution)/shard_map/all_gather | solution.py:40
  189.0 6.3 all-to-all-start
  195.4 0.0 reduce-scatter.2.cloned.1.call-start
  195.4 1.4 fusion.9
  196.8 0.1 reshape.65
  196.9 0.1 fusion.6
  197.1 0.6 scatter_custom_fusion
  197.7 135.7 %all-to-all-done = f32[4,768,1024]{2,1,0:T(8,128)} async-done(((f32[4,768,1024]{2,1,0:T(8,128)}), f32[4,768,1024]{2,1,0:T(8,128)}, u32[]{:S(2)}, u32[]{:S(2)}) %all-to-all-start) | async-done | bytes 12582944 | tf_op jit(solution)/shard_map/all_to_all | solution.py:41
  333.4 11.9 %copy.16 = f32[2,4,384,1024]{3,2,1,0:T(8,128)} copy(f32[2,4,384,1024]{3,2,0,1:T(8,128)} %bitcast.5) | data formatting | bytes 25165824 | tf_op jit(solution)/shard_map/transpose | solution.py:44
  345.3 3.4 broadcast_in_dim.8
  348.7 138.5 %while.12 = (s32[]{:T(128)}, f32[1536,1024]{1,0:T(8,128)}, s32[]{:T(128)}, s32[18]{0:T(128)S(1)}, f32[1536,3072]{1,0:T(8,128)}, /*index=5*/f32[3072,1024]{1,0:T(...) while((s32[]{:T(128)}, f32[1536,1024]{1,0:T(8,128)}, ...), condition=%wide.region_4.5_spmd, body=%wide.region_3.4_spmd.sunk | while | flops 3221749760 | bytes 7342482 | solution.py:60
  349.4 0.6 dynamic_slice.43
  351.9 7.5 add_dynamic-update-slice_fusion.2
  360.0 0.6 dynamic_slice.43
  362.5 7.5 add_dynamic-update-slice_fusion.2
  370.6 0.6 dynamic_slice.43
  373.1 7.5 add_dynamic-update-slice_fusion.2
  381.2 0.6 dynamic_slice.43
  383.7 7.5 add_dynamic-update-slice_fusion.2
  391.9 0.6 dynamic_slice.43
  394.4 7.5 add_dynamic-update-slice_fusion.2
  402.5 0.6 dynamic_slice.43
  405.0 7.4 add_dynamic-update-slice_fusion.2
  413.1 0.6 dynamic_slice.43
  415.6 7.4 add_dynamic-update-slice_fusion.2
  423.7 0.6 dynamic_slice.43
  426.1 7.4 add_dynamic-update-slice_fusion.2
  434.2 0.6 dynamic_slice.43
  436.7 7.5 add_dynamic-update-slice_fusion.2
  444.9 0.6 dynamic_slice.43
  447.3 7.5 add_dynamic-update-slice_fusion.2
  455.5 0.6 dynamic_slice.43
  457.9 7.5 add_dynamic-update-slice_fusion.2
  466.1 0.6 dynamic_slice.43
  468.6 7.5 add_dynamic-update-slice_fusion.2
  476.7 0.6 dynamic_slice.43
  479.2 7.5 add_dynamic-update-slice_fusion.2
  487.3 0.0 copy-start
  487.3 0.0 reduce-scatter.2.cloned.1.call-update
  487.3 0.0 all-reduce.2.cloned.1.call-start
  487.3 109.2 %reduce-scatter.2.cloned.1.call-done = f32[384,1024]{1,0:T(8,128)} async-done(((f32[1536,1024]{1,0:T(8,128)}), f32[384,1024]{1,0:T(8,128)}) %reduce-scatter.2.cloned.1.call-update) | async-done | bytes 1572880 | tf_op jit(solution)/shard_map/reduce_scatter | solution.py:62
  596.6 0.0 copy-done
  596.6 9.4 %convolution_bitcast_fusion = f32[1024,1024]{0,1:T(8,128)} fusion(f32[384,1024]{1,0:T(8,128)} %reduce-scatter.2.cloned.1.call-done, f32[384,1024]{1,0:T(8,128)S(1)} %copy-done), kind=kOutput, calls=%fused_computation.6 | convolution fusion | flops 4831838208 | bytes 7340032 | tf_op jit(solution)/shard_map/dot_general | solution.py:63
  606.0 0.0 all-reduce.2.cloned.1.call-update
  606.0 0.0 copy-start.1
  606.0 5.5 copy.17
  611.5 0.0 copy-done.1
  611.5 1.3 neg.3
  612.8 135.7 %all-reduce.2.cloned.1.call-done = f32[1024,1024]{0,1:T(8,128)} async-done(((f32[1024,1024]{0,1:T(8,128)}), f32[1024,1024]{0,1:T(8,128)}) %all-reduce.2.cloned.1.call-update) | async-done | bytes 4194320 | tf_op jit(solution)/shard_map/psum | solution.py:64
  748.5 6.8 add.78
  755.3 5.3 copy.18
  (2 shorter events, 0.0 us)
Async XLA Ops:
  7.2 181.8 %all-gather.2.cloned.1.call-start = ((), (), s32[]{:S(2)}) async-start(), calls=%async_computation.2 | async-start | bytes 14155776 | tf_op jit(solution)/shard_map/all_gather | solution.py:40
  189.0 144.4 %all-to-all-start = ((f32[4,768,1024]{2,1,0:T(8,128)}), f32[4,768,1024]{2,1,0:T(8,128)}, u32[]{:S(2)}, u32[]{:S(2)}) async-start(f32[4,768,1024]{2,1,0:T(8,128)} %bitcast.20), calls=%async_computation | async-start | bytes 25165824 | tf_op jit(solution)/shard_map/all_to_all | solution.py:41
  195.4 401.2 %reduce-scatter.2.cloned.1.call-start = ((), (), s32[]{:S(2)}) async-start(), calls=%async_computation.3 | async-start | bytes 7864320 | tf_op jit(solution)/shard_map/reduce_scatter | solution.py:62
  487.3 109.3 %copy-start = (f32[384,1024]{1,0:T(8,128)S(1)}, f32[384,1024]{1,0:T(8,128)}, u32[]{:S(2)}) copy-start(f32[384,1024]{1,0:T(8,128)} %param.8) | copy-start | bytes 4718596
  487.3 261.2 %all-reduce.2.cloned.1.call-start = ((), (), s32[]{:S(2)}) async-start(), calls=%async_computation.4 | async-start | bytes 8388608 | tf_op jit(solution)/shard_map/psum | solution.py:64
  606.0 5.5 copy-start.1
Sparse Core Ops, SparseCore 0:
  10.2 178.8 all-gather.1
  487.4 109.0 reduce-scatter.1
  606.1 142.2 all-reduce.1
where the time goes:
time: 768 us; the launch traced here: 767 us
  waiting for transfers between devices  562 us (73%)
  matrix products  106 us (14%)
  local copies, waits for them, and re-layouts  34.9 us (5%)
  loops' own time  33.6 us (4%)
  between operations  13.8 us (2%)
  other arithmetic  9.64 us (1%)
    all_gather x1, waiting for transfers between devices, body(): gathered = lax.all_gather(factor, 'row', axis=0, tiled=True)  181 us
    all_to_all x1, waiting for transfers between devices, body(): lax.all_to_all(gathered, 'col', split_axis=0, concat_axis=0, tiled=True)  136 us
    psum x1, waiting for transfers between devices, body(): diag_block = diag_inverse + lax.psum(outer_local, ('row', 'col'))  136 us
    reduce_scatter x1, waiting for transfers between devices, body(): lax.psum_scatter(partial_sum, 'col', scatter_dimension=0, tiled=True)  109 us
    dot_general x13, matrix products, add_product(): update = current + jnp.dot(inv_block, rows_part, precision=HIGHEST)  96.9 us
    another operation x1, loops' own time, body(): partial_sum = lax.fori_loop(0, mine_count, local_step, partial_sum)  33.6 us
  transfers between devices with their start and end apart: 4, of which 4 were waited for; matrix products, arithmetic and copies ran while one was open for 1% of the time, Pallas kernels for 0%

commit v1 on v0

v1 whole, which is shorter than its diff:
```python
import functools

import jax
import jax.numpy as jnp
from jax import lax
from jax.experimental import pallas as pl
from jax.experimental.pallas import tpu as pltpu
from jax.sharding import Mesh, PartitionSpec as P


B = 512
LANES = 128
SHARES = (1, 2, 2, 2, 1)
GROUPS = ((0,), (1, 2), (3, 4))
AHEAD = 2
OFFLOADED = (0,)
DEPTH = 4

CHIPS = ("z", "x", "y")
COLUMN = ("y", "k")
DEVICES = ("z", "x", "y", "k")
VMEM = pl.BlockSpec(memory_space=pltpu.VMEM)
SMEM = pl.BlockSpec(memory_space=pltpu.SMEM)
ANY = pl.BlockSpec(memory_space=pl.ANY)


def split(value):
    high = value.astype(jnp.bfloat16)
    low = (value - high.astype(jnp.float32)).astype(jnp.bfloat16)
    return high, low


def dot(left, right):
    return jnp.dot(left, right, preferred_element_type=jnp.float32)


def halve_kernel(tile_cols, tiles_ref, count_ref, inverse_ref, out_ref, held, made, sems, out_sems):
    count = count_ref[0]

    def fetch(step, slot):
        chosen = tiles_ref[step]
        row = pl.multiple_of(chosen // tile_cols * B, B)
        col = pl.multiple_of(chosen % tile_cols * B, B)
        return pltpu.make_async_copy(
            inverse_ref.at[pl.ds(row, B), pl.ds(col, B)], held.at[slot], sems.at[slot]
        )

    def put(step, slot):
        return pltpu.make_async_copy(made.at[slot], out_ref.at[step], out_sems.at[slot])

    for ahead in range(DEPTH - 1):

        @pl.when(ahead < count)
        def _():
            fetch(ahead, ahead).start()

    def step(index, carry):
        slot = lax.rem(index, DEPTH)
        side = lax.rem(index, 2)

        @pl.when(index + DEPTH - 1 < count)
        def _():
            fetch(index + DEPTH - 1, lax.rem(index + DEPTH - 1, DEPTH)).start()

        fetch(index, slot).wait()

        @pl.when(index >= 2)
        def _():
            put(index - 2, side).wait()

        high, low = split(held[slot])
        made[side, :, :B] = high
        made[side, :, B:] = low
        put(index, side).start()
        return carry

    lax.fori_loop(0, count, step, 0)
    for back in (2, 1):

        @pl.when(count >= back)
        def _():
            put(count - back, lax.rem(count - back, 2)).wait()


def halve(tiles, count, inverse):
    tile_rows, tile_cols = inverse.shape[0] // B, inverse.shape[1] // B
    return pl.pallas_call(
        functools.partial(halve_kernel, tile_cols),
        out_shape=jax.ShapeDtypeStruct((tile_rows * tile_cols, B, 2 * B), jnp.bfloat16),
        in_specs=[SMEM, SMEM, ANY],
        out_specs=ANY,
        scratch_shapes=[
            pltpu.VMEM((DEPTH, B, B), jnp.float32),
            pltpu.VMEM((2, B, 2 * B), jnp.bfloat16),
            pltpu.SemaphoreType.DMA((DEPTH,)),
            pltpu.SemaphoreType.DMA((2,)),
        ],
        cost_estimate=pl.CostEstimate(
            flops=0, bytes_accessed=8 * inverse.size, transcendentals=0
        ),
        name="halve",
    )(tiles, count, inverse)


def tiles_kernel(tile_cols, parts, tiles_ref, count_ref, place_ref, parts_ref, *refs):
    part_refs = refs[:parts]
    keep_ref, send_ref, highs, lows, total, held, came, sems, came_sems, out_sems = refs[parts:]
    count = count_ref[0]
    x, z, k = place_ref[0], place_ref[1], place_ref[2]
    cols, rows_each = part_refs[0].shape[0], part_refs[0].shape[1]

    def fetch(step, slot):
        return pltpu.make_async_copy(parts_ref.at[step], held.at[slot], sems.at[slot])

    for ahead in range(DEPTH - 1):

        @pl.when(ahead < count)
        def _():
            fetch(ahead, ahead).start()

    arrivals = [
        pltpu.make_async_copy(part_ref, came.at[index], came_sems.at[index])
        for index, part_ref in enumerate(part_refs)
    ]
    for arrival in arrivals:
        arrival.start()
    total[...] = jnp.zeros_like(total)
    for index in range(parts):
        half = lax.bitwise_xor(x, index) if parts == 2 else 0
        arrivals[index].wait()
        for j in range(cols):
            origin = lax.rem(z + j, cols)
            first = pl.multiple_of((half * cols + origin) * rows_each, rows_each)
            high, low = split(came[index, j])
            highs[pl.ds(first, rows_each), :] = high
            lows[pl.ds(first, rows_each), :] = low

    def step(index, carry):
        slot = lax.rem(index, DEPTH)

        @pl.when(index + DEPTH - 1 < count)
        def _():
            fetch(index + DEPTH - 1, lax.rem(index + DEPTH - 1, DEPTH)).start()

        fetch(index, slot).wait()
        chosen = tiles_ref[index]
        row = pl.multiple_of(chosen // tile_cols * B, B)
        col = pl.multiple_of(chosen % tile_cols * B, B)
        high, low = highs[pl.ds(col, B), :], lows[pl.ds(col, B), :]
        width = total.shape[1]
        if width == LANES:
            both = dot(held[slot, :, :B], jnp.concatenate([high, low], axis=1))
            product = both[:, :width] + both[:, width:] + dot(held[slot, :, B:], high)
        else:
            product = (
                dot(held[slot, :, :B], high)
                + dot(held[slot, :, B:], high)
                + dot(held[slot, :, :B], low)
            )
        total[pl.ds(row, B), :] += product
        return carry

    lax.fori_loop(0, count, step, 0)
    pairs, rows_out = keep_ref.shape[0], keep_ref.shape[1]
    copies = []
    for index, (out_ref, side) in enumerate(((send_ref, 1 - k), (keep_ref, k))):
        for pair in range(pairs):
            first = pl.multiple_of((2 * pair + side) * rows_out, rows_out)
            copies.append(
                pltpu.make_async_copy(
                    total.at[pl.ds(first, rows_out), :],
                    out_ref.at[pair],
                    out_sems.at[index * pairs + pair],
                )
            )
    for copy in copies:
        copy.start()
    for copy in copies:
        copy.wait()


def tile_products(tiles, count, place, halved, parts, rows, tile_cols):
    cols, _, width = parts[0].shape
    out = jax.ShapeDtypeStruct((cols // 2, rows // cols, width), jnp.float32)
    return pl.pallas_call(
        functools.partial(tiles_kernel, tile_cols, len(parts)),
        out_shape=(out, out),
        in_specs=[SMEM, SMEM, SMEM, ANY] + [ANY] * len(parts),
        out_specs=(ANY, ANY),
        scratch_shapes=[
            pltpu.VMEM((tile_cols * B, width), jnp.bfloat16),
            pltpu.VMEM((tile_cols * B, width), jnp.bfloat16),
            pltpu.VMEM((rows, width), jnp.float32),
            pltpu.VMEM((DEPTH, B, 2 * B), jnp.bfloat16),
            pltpu.VMEM((len(parts), *parts[0].shape), jnp.float32),
            pltpu.SemaphoreType.DMA((DEPTH,)),
            pltpu.SemaphoreType.DMA((len(parts),)),
            pltpu.SemaphoreType.DMA((cols,)),
        ],
        cost_estimate=pl.CostEstimate(
            flops=6 * rows * tile_cols * B * width,
            bytes_accessed=4 * rows * tile_cols * B,
            transcendentals=0,
        ),
        name="tiles",
    )(tiles, count, place, halved, *parts)


def turn_kernel(pairs, place_ref, *refs):
    out_ref = refs[-1]
    for index in range(pairs):
        value = refs[index][...] if pairs == 2 else refs[0][index]
        rows = value.shape[0]
        if pairs == 2:
            side = lax.bitwise_xor(place_ref[3], index)
            where = pl.ds(pl.multiple_of(side * rows, rows), rows)
        else:
            where = slice(index * rows, (index + 1) * rows)
        high, low = split(value.T)
        out_ref[0, :, where] = high
        out_ref[1, :, where] = low


def turn(place, factors, pairs, rows, width):
    return pl.pallas_call(
        functools.partial(turn_kernel, pairs),
        out_shape=jax.ShapeDtypeStruct((2, width, pairs * rows), jnp.bfloat16),
        in_specs=[SMEM] + [VMEM] * len(factors),
        out_specs=VMEM,
        name="turn",
    )(place, *factors)


def finish_kernel(swapped, place_ref, kept_ref, came_ref, turned_ref, sum_ref, term_ref):
    pairs, rows, width = kept_ref.shape
    for pair in range(pairs):
        sum_ref[pair] = kept_ref[pair] + came_ref[pair]
    high, low = split(sum_ref[...].reshape(pairs * rows, width))
    half = term_ref.shape[1]
    for index in range(2):
        side = lax.bitwise_xor(place_ref[2], index) if swapped else index
        left = pl.ds(pl.multiple_of(side * half, half), half)
        term_ref[index] = (
            dot(turned_ref[0, left, :], high)
            + dot(turned_ref[1, left, :], high)
            + dot(turned_ref[0, left, :], low)
        )


def finish(place, kept, came, turned, swapped):
    pairs, rows, step = kept.shape
    width = turned.shape[1]
    return pl.pallas_call(
        functools.partial(finish_kernel, swapped),
        out_shape=(
            jax.ShapeDtypeStruct(kept.shape, jnp.float32),
            jax.ShapeDtypeStruct((2, width // 2, step), jnp.float32),
        ),
        in_specs=[SMEM, VMEM, VMEM, VMEM],
        out_specs=(VMEM, VMEM),
        cost_estimate=pl.CostEstimate(
            flops=6 * pairs * rows * width * step,
            bytes_accessed=4 * pairs * rows * (width + 3 * step) + 4 * width * step,
            transcendentals=0,
        ),
        name="finish",
    )(place, kept, came, turned)


def stored_list(pattern, first_row, first_col, tile_rows, tile_cols):
    window = lax.dynamic_slice(pattern, (first_row, first_col), (tile_rows, tile_cols)).reshape(-1)
    count_all = tile_rows * tile_cols
    order = jnp.cumsum(window) - 1
    slots = jnp.arange(count_all, dtype=jnp.int32)
    chosen = (order[None, :] == slots[:, None]) & (window[None, :] > 0)
    return jnp.sum(jnp.where(chosen, slots[None, :], 0), axis=1), jnp.sum(window)[None]


def swap(value, axis):
    return lax.ppermute(value, axis, [(0, 1), (1, 0)])


def sum_scatter(value, axes):
    return jnp.sum(lax.all_to_all(value, axes, split_axis=0, concat_axis=0), axis=0)


def spread(value, axes):
    copies = jnp.broadcast_to(value[None], (lax.axis_size(axes), *value.shape))
    return lax.all_to_all(copies, axes, split_axis=0, concat_axis=0)


def pick(pair, index):
    return lax.dynamic_index_in_dim(pair, index, 0, False)


def routes(planes, cols, turn_index):
    ratio = 2 * planes // cols
    pairs = []
    for z in range(planes):
        for x in range(2):
            for col in range(cols):
                if ratio == 1 and col % 2 != x:
                    continue
                source = ((col * ratio // 2) * 2 + x) * cols + (z + turn_index) % cols
                pairs.append((source, (z * 2 + x) * cols + col))
    return pairs


def shares(width):
    return SHARES if sum(SHARES) * LANES == width else (1,) * (width // LANES)


def after(value, others):
    return lax.optimization_barrier((value, others))[0]


def step_body(inverse, pattern, factor, diag_inverse):
    planes, cols = lax.axis_size("z"), lax.axis_size(COLUMN)
    x, y, z, k = (lax.axis_index(a) for a in ("x", "y", "z", "k"))
    column = lax.axis_index(COLUMN)
    ratio = 2 * planes // cols
    rows_each, width = factor.shape
    tile_rows, tile_cols = inverse.shape[0] // B, inverse.shape[1] // B
    tiles, count = stored_list(
        pattern, (z * 2 + x) * tile_rows, column * tile_cols, tile_rows, tile_cols
    )
    place = jnp.stack([x, z, k, y]).astype(jnp.int32)
    chips = lax.axis_size(CHIPS)
    pairs = cols // 2
    if pairs == 2:
        factors = (factor, swap(factor, "y"))
    else:
        factors = (lax.all_gather(factor, "y", axis=0),)
    halved = halve(tiles, count, inverse)
    turned = turn(place, factors, pairs, rows_each, width)
    arrivals, panels, terms = [], [], []
    pieces, spreads, pending, diags = {}, {}, {}, {}
    first = 0
    groups = groups_of(len(shares(width)))
    for chunk, share in enumerate(shares(width)):
        step = share * LANES
        part = factor[:, first : first + step]
        first += step
        if chunk >= AHEAD:
            part = after(part, arrivals[chunk - AHEAD])
        mine = []
        for j in range(cols):
            mine.append(lax.ppermute(part, DEVICES, routes(planes, cols, j)))
        arrivals.append(mine)
        mine = jnp.stack(mine)
        theirs = swap(mine, "x")
        parts = (mine, theirs) if ratio == 2 else (jnp.where(column % 2 == x, mine, theirs),)
        gate = after(place, pieces[chunk - 2]) if chunk - 2 in pieces else place
        kept, send = tile_products(tiles, count, gate, halved, parts, inverse.shape[0], tile_cols)
        for index, (born, state, value) in list(pending.items()):
            value = after(value, kept)
            if state == 0:
                piece = jnp.sum(value, axis=0)
                pieces[chunk - 1] = piece
                pending[index] = (born, 1, spread(piece, CHIPS))
            else:
                spreads[born] = value
                del pending[index]
                diags[index] = assemble(value, width, k)
        came = swap(send, "k")
        gate = after(place, spreads[chunk - 2]) if chunk - 2 in spreads else place
        summed, term = finish(gate, kept, came, turned, chunk not in groups[0])
        terms.append(term)
        if pairs == 2:
            panels.append(-(pick(summed, y) + swap(pick(summed, 1 - y), "y")))
        else:
            panels.append(-sum_scatter(summed, "y"))
        for index, group in enumerate(groups):
            if not group or group[-1] != chunk:
                continue
            mine = [terms[member] for member in group]
            if index in OFFLOADED:
                diags[index] = lax.psum([term.reshape(width, -1) for term in mine], DEVICES)
                continue
            half = jnp.concatenate([term[0] for term in mine], 1) + swap(
                jnp.concatenate([term[1] for term in mine], 1), "k"
            )
            sent = half.reshape(chips, -1, half.shape[1])
            value = lax.all_to_all(sent, CHIPS, split_axis=0, concat_axis=0)
            pending[index] = (chunk, 0, value)
    for index, (_, state, value) in sorted(pending.items()):
        if state == 0:
            value = spread(jnp.sum(value, axis=0), CHIPS)
        diags[index] = assemble(value, width, k)
    diags = [piece for index in sorted(diags) for piece in diags[index]]
    return jnp.concatenate(panels, 1), diag_inverse + jnp.concatenate(diags, 1)


def assemble(value, width, k):
    full = value.reshape(width // 2, -1)
    far = swap(full, "k")
    return [jnp.concatenate([jnp.where(k == 0, full, far), jnp.where(k == 0, far, full)], 0)]


def groups_of(chunks):
    return GROUPS if chunks == len(SHARES) else ((), tuple(range(chunks)))


def solution(mesh):
    rows, cols = mesh.shape["row"], mesh.shape["col"]
    grid = Mesh(mesh.devices.reshape(rows // 2, 2, cols // 2, 2), DEVICES)
    return jax.shard_map(
        step_body,
        mesh=grid,
        in_specs=(P(("z", "x"), ("y", "k")), P(), P(DEVICES, None), P()),
        out_specs=(P(DEVICES, None), P()),
        check_vma=False,
    )
```

time: 768 us -> 581 us (0.76)
  waiting for transfers between devices: 562 us -> 240 us
  starting transfers between devices: 6.46 us -> 198 us
  matrix products: 106 us -> 0 us
  Pallas kernels: 0 us -> 86.7 us
  loops' own time: 33.6 us -> 0 us
  local copies, waits for them, and re-layouts: 34.9 us -> 19.6 us
  other arithmetic: 9.64 us -> 20.3 us
    all_gather x1 -> x0, waiting for transfers between devices: 181 us -> none  [body(): gathered = lax.all_gather(factor, 'row', axis=0, tiled=True)]
    ppermute x0 -> x40, waiting for transfers between devices: none -> 156 us  [the longest x20 100 us: swap(): return lax.ppermute(value, axis, [(0, 1), (1, 0)])]
    all_to_all x1 -> x4, waiting for transfers between devices: 136 us -> 0.01 us  [the longest x2 0.01 us: step_body(): value = lax.all_to_all(sent, CHIPS, split_axis=0, concat_axis=0)]
    ppermute x0 -> x40, starting transfers between devices: none -> 134 us  [the longest x20 93.6 us: step_body(): mine.append(lax.ppermute(part, DEVICES, routes(planes, cols, j)))]
    reduce_scatter x1 -> x0, waiting for transfers between devices: 109 us -> none  [body(): lax.psum_scatter(partial_sum, 'col', scatter_dimension=0, tiled=True)]
    dot_general x14 -> x0, matrix products: 106 us -> none  [the longest x13 96.9 us: add_product(): update = current + jnp.dot(inv_block, rows_part, precision=HIGHEST)]
    pallas_call x0 -> x12, Pallas kernels: none -> 86.7 us  [the longest x5 50.6 us: tile_products(): pl.pallas_call(functools.partial(tiles_kernel, tile_cols, len(parts)), ou...]
    all_to_all x1 -> x4, starting transfers between devices: 6.34 us -> 64.4 us  [the longest x2 36.5 us: step_body(): value = lax.all_to_all(sent, CHIPS, split_axis=0, concat_axis=0)]
  transfers between devices with their start and end apart: 4 -> 45, of which waited for: 4 -> 18; matrix products, arithmetic and copies ran while one was open for 1% -> 4% of each run, Pallas kernels for 0% -> 13%
where the time goes in v1:
time: 581 us; the launch traced here: 580 us
  waiting for transfers between devices  240 us (41%)
  starting transfers between devices  198 us (34%)
  Pallas kernels  86.7 us (15%)
  other arithmetic  20.3 us (3%)
  local copies, waits for them, and re-layouts  19.6 us (3%)
  between operations  14.6 us (3%)
    ppermute x20, waiting for transfers between devices, swap(): return lax.ppermute(value, axis, [(0, 1), (1, 0)])  100 us
    ppermute x20, starting transfers between devices, step_body(): mine.append(lax.ppermute(part, DEVICES, routes(planes, cols, j)))  93.6 us
    psum x1, waiting for transfers between devices, step_body(): diags[index] = lax.psum([term.reshape(width, -1) for term in mine], DEVICES)  84.4 us
    ppermute x20, waiting for transfers between devices, step_body(): mine.append(lax.ppermute(part, DEVICES, routes(planes, cols, j)))  55.6 us
    pallas_call x5, Pallas kernels, tile_products(): pl.pallas_call(functools.partial(tiles_kernel, tile_cols, len(parts)), ou...  50.6 us
    ppermute x20, starting transfers between devices, swap(): return lax.ppermute(value, axis, [(0, 1), (1, 0)])  40.1 us
    all_to_all x2, starting transfers between devices, step_body(): value = lax.all_to_all(sent, CHIPS, split_axis=0, concat_axis=0)  36.5 us
    all_to_all x2, starting transfers between devices, spread(): return lax.all_to_all(copies, axes, split_axis=0, concat_axis=0)  27.9 us
  transfers between devices with their start and end apart: 45, of which 18 were waited for; matrix products, arithmetic and copies ran while one was open for 4% of the time, Pallas kernels for 13%

profile of v1, /device:TPU:0, one launch (start us, length us, event | category | flops | bytes accessed | tf_op | source)
XLA Modules:
  0.0 579.5 jit_solution(12322527854892896746)
XLA Ops:
  7.2 1.4 fusion.13
  9.3 7.0 %collective-permute-start.9 = (f32[384,256]{1,0:T(8,128)S(1)}, f32[384,256]{1,0:T(8,128)S(1)}, u32[]{:S(2)}, u32[]{:S(2)}) collective-permute-start(f32[384,256]{1,0:T(8,128)S(1)} %get-tuple-element.66), channel_id=1, source_target_pairs={{1,0},{9,1},{17,2},{25,3},{5,4},{13,5},{21,6},{29,7},{2,8},{10,9},... | collective-permute-start | bytes 1179656 | tf_op jit(solution)/shard_map/ppermute | solution.py:348
  17.2 1.6 collective-permute-start.11
  20.1 9.6 %collective-permute-start.1 = (f32[384,128]{1,0:T(8,128)S(1)}, f32[384,128]{1,0:T(8,128)S(1)}, u32[]{:S(2)}, u32[]{:S(2)}) collective-permute-start(f32[384,128]{1,0:T(8,128)S(1)} %get-tuple-element.63), channel_id=1, source_target_pairs={{1,0},{9,1},{17,2},{25,3},{5,4},{13,5},{21,6},{29,7},{2,8},{10,9},... | collective-permute-start | bytes 589832 | tf_op jit(solution)/shard_map/ppermute | solution.py:348
  29.7 11.6 %collective-permute-start.2 = (f32[384,128]{1,0:T(8,128)S(1)}, f32[384,128]{1,0:T(8,128)S(1)}, u32[]{:S(2)}, u32[]{:S(2)}) collective-permute-start(f32[384,128]{1,0:T(8,128)S(1)} %get-tuple-element.63), channel_id=1, source_target_pairs={{2,0},{10,1},{18,2},{26,3},{6,4},{14,5},{22,6},{30,7},{3,8},{11,9}... | collective-permute-start | bytes 589832 | tf_op jit(solution)/shard_map/ppermute | solution.py:348
  41.4 17.5 %collective-permute-start.3 = (f32[384,128]{1,0:T(8,128)S(1)}, f32[384,128]{1,0:T(8,128)S(1)}, u32[]{:S(2)}, u32[]{:S(2)}) collective-permute-start(f32[384,128]{1,0:T(8,128)S(1)} %get-tuple-element.63), channel_id=1, source_target_pairs={{3,0},{11,1},{19,2},{27,3},{7,4},{15,5},{23,6},{31,7},{0,8},{8,9},... | collective-permute-start | bytes 589832 | tf_op jit(solution)/shard_map/ppermute | solution.py:348
  59.0 1.6 collective-permute-start.12
  60.6 1.6 collective-permute-done.2
  62.9 6.9 %collective-permute-start.16 = (f32[384,256]{1,0:T(8,128)S(1)}, f32[384,256]{1,0:T(8,128)S(1)}, u32[]{:S(2)}, u32[]{:S(2)}) collective-permute-start(f32[384,256]{1,0:T(8,128)S(1)} %get-tuple-element.35), channel_id=1, source_target_pairs={{1,0},{9,1},{17,2},{25,3},{5,4},{13,5},{21,6},{29,7},{2,8},{10,9},... | collective-permute-start | bytes 1179656 | tf_op jit(solution)/shard_map/ppermute | solution.py:348
  69.8 3.9 collective-permute-start.17
  74.0 5.3 collective-permute-done.16
  79.3 9.6 %collective-permute-done.17 = f32[384,256]{1,0:T(8,128)S(1)} collective-permute-done((f32[384,256]{1,0:T(8,128)S(1)}, f32[384,256]{1,0:T(8,128)S(1)}, u32[]{:S(2)}, u32[]{:S(2)}) %collective-permute-start.17) | collective-permute-done | bytes 393248 | tf_op jit(solution)/shard_map/ppermute | solution.py:348
  89.0 5.1 collective-permute-done.18
  94.0 1.2 pad_maximum_fusion.1.refs_0_
  95.3 1.6 collective-permute-start.19
  96.8 16.3 %collective-permute-start.6 = (f32[384,1024]{1,0:T(8,128)S(1)}, f32[384,1024]{1,0:T(8,128)}, u32[]{:S(2)}, u32[]{:S(2)}) collective-permute-start(f32[384,1024]{1,0:T(8,128)S(1)} %copy-done), channel_id=1, source_target_pairs={{0,2},{2,0},{1,3},{3,1},{4,6},{6,4},{5,7},{7,5},{8,10},{10,8},{9,1... | collective-permute-start | bytes 4718600 | tf_op jit(solution)/shard_map/ppermute | solution.py:280
  113.1 1.5 fusion.11
  118.2 8.7 %halve.1.parts_ref = bf16[18,512,1024]{2,1,0:T(8,128)(2,1)} custom-call(s32[18]{0:T(128)} %select_reduce_fusion.tiles_ref, s32[1]{0:T(128)} %bitcast.4.count_ref, f32[1536,3072]{1,0:T(8,128)} %inverse_ref.1), custom_call_target="tpu_custom_call" | custom-call | bytes 37748736 | tf_op jit(solution)/shard_map/halve/pallas_call | solution.py:87
  127.6 11.0 %tiles.6 = (f32[2,384,256]{2,1,0:T(8,128)}, f32[2,384,256]{2,1,0:T(8,128)}) custom-call(s32[18]{0:T(128)} %select_reduce_fusion.tiles_ref, s32[1]{0:T(128)} %bitcast.4.count_ref, s32[4]{0:T(128)} %pad_add_fusion.place_ref, bf16[18,512,1024]{2,1,0:T(8,128)(2,1)} %halve.1.parts_ref, f32[4,384,256]{2,1,0:T(8,128)} %copy-done.3, ...), custom_call_target="tpu_custom_call" | custom-call | flops 7247757312 | bytes 18874368 | tf_op jit(solution)/shard_map/tiles/pallas_call | solution.py:185
  138.6 10.9 %tiles.7 = (f32[2,384,256]{2,1,0:T(8,128)}, f32[2,384,256]{2,1,0:T(8,128)}) custom-call(s32[18]{0:T(128)} %select_reduce_fusion.tiles_ref, s32[1]{0:T(128)} %bitcast.4.count_ref, s32[4]{0:T(128)} %pad_add_fusion.place_ref, bf16[18,512,1024]{2,1,0:T(8,128)(2,1)} %halve.1.parts_ref, f32[4,384,256]{2,1,0:T(8,128)} %pad_maximum_fusion.1.refs_0_, ...), custom_call_target="tpu_custom_call" | custom-call | flops 7247757312 | bytes 18874368 | tf_op jit(solution)/shard_map/tiles/pallas_call | solution.py:185
  149.6 4.4 turn.1.turned_ref
  155.0 4.7 finish.6
  159.7 1.3 slice_bitcast_fusion.5
  161.9 4.7 finish.7
  166.6 1.3 slice_bitcast_fusion.4
  169.3 6.0 %collective-permute-start.23 = (f32[384,256]{1,0:T(8,128)S(1)}, f32[384,256]{1,0:T(8,128)S(1)}, u32[]{:S(2)}, u32[]{:S(2)}) collective-permute-start(f32[384,256]{1,0:T(8,128)S(1)} %get-tuple-element.39), channel_id=1, source_target_pairs={{1,0},{9,1},{17,2},{25,3},{5,4},{13,5},{21,6},{29,7},{2,8},{10,9},... | collective-permute-start | bytes 1179656 | tf_op jit(solution)/shard_map/ppermute | solution.py:348
  175.3 11.7 %collective-permute-start.24 = (f32[384,256]{1,0:T(8,128)S(1)}, f32[384,256]{1,0:T(8,128)S(1)}, u32[]{:S(2)}, u32[]{:S(2)}) collective-permute-start(f32[384,256]{1,0:T(8,128)S(1)} %get-tuple-element.39), channel_id=1, source_target_pairs={{2,0},{10,1},{18,2},{26,3},{6,4},{14,5},{22,6},{30,7},{3,8},{11,9}... | collective-permute-start | bytes 1179656 | tf_op jit(solution)/shard_map/ppermute | solution.py:348
  187.0 4.0 collective-permute-start.25
  191.0 15.3 %collective-permute-done.24 = f32[384,256]{1,0:T(8,128)S(1)} collective-permute-done((f32[384,256]{1,0:T(8,128)S(1)}, f32[384,256]{1,0:T(8,128)S(1)}, u32[]{:S(2)}, u32[]{:S(2)}) %collective-permute-start.24) | collective-permute-done | bytes 393248 | tf_op jit(solution)/shard_map/ppermute | solution.py:348
  206.4 6.7 %collective-permute-start.26 = (f32[4,384,256]{2,1,0:T(8,128)S(1)}, f32[4,384,256]{2,1,0:T(8,128)}, u32[]{:S(2)}, u32[]{:S(2)}) collective-permute-start(f32[4,384,256]{2,1,0:T(8,128)S(1)} %pad_maximum_fusion.2.refs_0_), channel_id=1, source_target_pairs={{0,4},{4,0},{1,5},{5,1},{2,6},{6,2},{3,7},{7,3},{8,12},{12,8},{9,1... | collective-permute-start | bytes 4718600 | tf_op jit(solution)/shard_map/ppermute | solution.py:280
  214.3 15.1 %all-to-all-start = ((f32[16,32,512]{2,1,0:T(8,128)}), f32[16,32,512]{2,1,0:T(8,128)S(1)}, u32[]{:S(2)}, u32[]{:S(2)}) async-start(f32[16,32,512]{2,1,0:T(8,128)} %bitcast.33), calls=%async_computation | async-start | bytes 2097152 | tf_op jit(solution)/shard_map/all_to_all | solution.py:384
  229.4 23.6 %collective-permute-done.26.refs_1_ = f32[4,384,256]{2,1,0:T(8,128)} collective-permute-done((f32[4,384,256]{2,1,0:T(8,128)S(1)}, f32[4,384,256]{2,1,0:T(8,128)}, u32[]{:S(2)}, u32[]{:S(2)}) %collective-permute-start.26) | collective-permute-done | bytes 1572896 | tf_op jit(solution)/shard_map/ppermute | solution.py:280
  253.0 10.9 %tiles.8 = (f32[2,384,256]{2,1,0:T(8,128)}, f32[2,384,256]{2,1,0:T(8,128)}) custom-call(s32[18]{0:T(128)} %select_reduce_fusion.tiles_ref, s32[1]{0:T(128)} %bitcast.4.count_ref, s32[4]{0:T(128)} %pad_add_fusion.place_ref, bf16[18,512,1024]{2,1,0:T(8,128)(2,1)} %halve.1.parts_ref, f32[4,384,256]{2,1,0:T(8,128)} %copy-done.4, ...), custom_call_target="tpu_custom_call" | custom-call | flops 7247757312 | bytes 18874368 | tf_op jit(solution)/shard_map/tiles/pallas_call | solution.py:185
  265.2 18.2 %all-to-all-start.1 = ((f32[16,32,512]{2,1,0:T(8,128)}), f32[16,32,512]{2,1,0:T(8,128)S(1)}, u32[]{:S(2)}, u32[]{:S(2)}) async-start(f32[16,32,512]{2,1,0:T(8,128)} %broadcast_in_dim.33), calls=%async_computation.1 | async-start | bytes 2097152 | tf_op jit(solution)/shard_map/all_to_all | solution.py:289
  284.1 8.6 %collective-permute-start.31 = (f32[384,128]{1,0:T(8,128)S(1)}, f32[384,128]{1,0:T(8,128)S(1)}, u32[]{:S(2)}, u32[]{:S(2)}) collective-permute-start(f32[384,128]{1,0:T(8,128)S(1)} %copy-done.26), channel_id=1, source_target_pairs={{1,0},{9,1},{17,2},{25,3},{5,4},{13,5},{21,6},{29,7},{2,8},{10,9},... | collective-permute-start | bytes 589832 | tf_op jit(solution)/shard_map/ppermute | solution.py:348
  293.3 10.3 %collective-permute-done.31 = f32[384,128]{1,0:T(8,128)S(1)} collective-permute-done((f32[384,128]{1,0:T(8,128)S(1)}, f32[384,128]{1,0:T(8,128)S(1)}, u32[]{:S(2)}, u32[]{:S(2)}) %collective-permute-start.31) | collective-permute-done | bytes 196640 | tf_op jit(solution)/shard_map/ppermute | solution.py:348
  303.6 8.0 %collective-permute-done.32 = f32[384,128]{1,0:T(8,128)S(1)} collective-permute-done((f32[384,128]{1,0:T(8,128)S(1)}, f32[384,128]{1,0:T(8,128)S(1)}, u32[]{:S(2)}, u32[]{:S(2)}) %collective-permute-start.32) | collective-permute-done | bytes 196640 | tf_op jit(solution)/shard_map/ppermute | solution.py:348
  312.1 2.5 collective-permute-start.34
  314.5 1.6 collective-permute-start.27
  316.1 15.8 %collective-permute-done.34.refs_1_ = f32[4,384,128]{2,1,0:T(8,128)S(1)} collective-permute-done((f32[4,384,128]{2,1,0:T(8,128)S(1)}, f32[4,384,128]{2,1,0:T(8,128)S(1)}, u32[]{:S(2)}, u32[]{:S(2)}) %collective-permute-start.34) | collective-permute-done | bytes 786464 | tf_op jit(solution)/shard_map/ppermute | solution.py:280
  332.9 9.0 %tiles.9 = (f32[2,384,128]{2,1,0:T(8,128)}, f32[2,384,128]{2,1,0:T(8,128)}) custom-call(s32[18]{0:T(128)} %select_reduce_fusion.tiles_ref, s32[1]{0:T(128)} %bitcast.4.count_ref, s32[4]{0:T(128)} %pad_add_fusion.place_ref, bf16[18,512,1024]{2,1,0:T(8,128)(2,1)} %halve.1.parts_ref, f32[4,384,128]{2,1,0:T(8,128)} %copy-done.1, f32[4,384,128]{2,1,0:T(8,128)} %copy-done.5), custom_call_target="tpu_custom_call" | custom-call | flops 3623878656 | bytes 18874368 | tf_op jit(solution)/shard_map/tiles/pallas_call | solution.py:185
  343.2 4.7 finish.8
  347.9 1.3 slice_bitcast_fusion.1
  350.0 4.3 finish.9
  355.6 2.1 collective-permute-done.38
  358.8 21.4 %all-to-all-start.2 = ((f32[16,32,384]{2,1,0:T(8,128)}), f32[16,32,384]{2,1,0:T(8,128)S(1)}, u32[]{:S(2)}, u32[]{:S(2)}) async-start(f32[16,32,384]{2,1,0:T(8,128)} %bitcast.46), calls=%async_computation.2 | async-start | bytes 1572864 | tf_op jit(solution)/shard_map/all_to_all | solution.py:384
  380.3 2.0 collective-permute-start.4
  382.2 25.7 %collective-permute-done.4.refs_1_ = f32[4,384,128]{2,1,0:T(8,128)S(1)} collective-permute-done((f32[4,384,128]{2,1,0:T(8,128)S(1)}, f32[4,384,128]{2,1,0:T(8,128)S(1)}, u32[]{:S(2)}, u32[]{:S(2)}) %collective-permute-start.4) | collective-permute-done | bytes 786464 | tf_op jit(solution)/shard_map/ppermute | solution.py:280
  408.9 8.8 %tiles.5 = (f32[2,384,128]{2,1,0:T(8,128)}, f32[2,384,128]{2,1,0:T(8,128)}) custom-call(s32[18]{0:T(128)} %select_reduce_fusion.tiles_ref, s32[1]{0:T(128)} %bitcast.4.count_ref, s32[4]{0:T(128)} %pad_add_fusion.place_ref, bf16[18,512,1024]{2,1,0:T(8,128)(2,1)} %halve.1.parts_ref, f32[4,384,128]{2,1,0:T(8,128)} %copy-done.2, f32[4,384,128]{2,1,0:T(8,128)} %copy-done.6), custom_call_target="tpu_custom_call" | custom-call | flops 3623878656 | bytes 18874368 | tf_op jit(solution)/shard_map/tiles/pallas_call | solution.py:185
  418.8 9.7 %all-to-all-start.3 = ((f32[16,32,384]{2,1,0:T(8,128)}), f32[16,32,384]{2,1,0:T(8,128)}, u32[]{:S(2)}, u32[]{:S(2)}) async-start(f32[16,32,384]{2,1,0:T(8,128)} %broadcast_in_dim.34), calls=%async_computation.3 | async-start | bytes 1572864 | tf_op jit(solution)/shard_map/all_to_all | solution.py:289
  429.4 4.4 finish.5
  434.9 1.9 collective-permute-start.7
  437.1 1.9 collective-permute-start.21
  439.0 9.2 %collective-permute-done.7 = f32[384,128]{1,0:T(8,128)S(1)} collective-permute-done((f32[384,128]{1,0:T(8,128)S(1)}, f32[384,128]{1,0:T(8,128)S(1)}, u32[]{:S(2)}, u32[]{:S(2)}) %collective-permute-start.7) | collective-permute-done | bytes 196640 | tf_op jit(solution)/shard_map/ppermute | solution.py:280
  449.1 1.5 collective-permute-start.28
  450.5 6.9 %collective-permute-done.14 = f32[384,256]{1,0:T(8,128)S(1)} collective-permute-done((f32[384,256]{1,0:T(8,128)S(1)}, f32[384,256]{1,0:T(8,128)S(1)}, u32[]{:S(2)}, u32[]{:S(2)}) %collective-permute-start.14) | collective-permute-done | bytes 393248 | tf_op jit(solution)/shard_map/ppermute | solution.py:280
  457.5 8.4 %collective-permute-done.21 = f32[384,256]{1,0:T(8,128)S(1)} collective-permute-done((f32[384,256]{1,0:T(8,128)S(1)}, f32[384,256]{1,0:T(8,128)S(1)}, u32[]{:S(2)}, u32[]{:S(2)}) %collective-permute-start.21) | collective-permute-done | bytes 393248 | tf_op jit(solution)/shard_map/ppermute | solution.py:280
  468.1 6.7 %collective-permute-done.28 = f32[384,256]{1,0:T(8,128)} collective-permute-done((f32[384,256]{1,0:T(8,128)}, f32[384,256]{1,0:T(8,128)}, u32[]{:S(2)}, u32[]{:S(2)}) %collective-permute-start.28) | collective-permute-done | bytes 393248 | tf_op jit(solution)/shard_map/ppermute | solution.py:280
  474.8 1.8 fusion.1
  476.6 1.6 collective-permute-done.36
  478.9 1.6 broadcast_select_fusion.1
  480.4 2.2 broadcast_select_fusion.3
  482.6 84.4 %all-reduce.2.cloned.1.call-done = f32[1024,128]{1,0:T(8,128)} async-done(((f32[1024,128]{1,0:T(8,128)}), f32[1024,128]{1,0:T(8,128)}) %all-reduce.2.cloned.1.call-update) | async-done | bytes 524304 | tf_op jit(solution)/shard_map/psum | solution.py:378
  567.1 5.6 maximum_add_fusion
  (135 shorter events, 29.0 us)
Async XLA Ops:
  7.2 11.6 %copy-start = (f32[384,1024]{1,0:T(8,128)S(1)}, f32[384,1024]{1,0:T(8,128)}, u32[]{:S(2)}) copy-start(f32[384,1024]{1,0:T(8,128)} %refs_0_.1) | copy-start | bytes 4718596
  8.6 11.5 %collective-permute-start.8 = (f32[384,256]{1,0:T(8,128)S(1)}, f32[384,256]{1,0:T(8,128)S(1)}, u32[]{:S(2)}, u32[]{:S(2)}) collective-permute-start(f32[384,256]{1,0:T(8,128)S(1)} %get-tuple-element.66), channel_id=1, source_target_pairs={{0,0},{8,1},{16,2},{24,3},{4,4},{12,5},{20,6},{28,7},{1,8},{9,9},{... | collective-permute-start | bytes 1179656 | tf_op jit(solution)/shard_map/ppermute | solution.py:348
  9.3 20.4 %collective-permute-start.9 = (f32[384,256]{1,0:T(8,128)S(1)}, f32[384,256]{1,0:T(8,128)S(1)}, u32[]{:S(2)}, u32[]{:S(2)}) collective-permute-start(f32[384,256]{1,0:T(8,128)S(1)} %get-tuple-element.66), channel_id=1, source_target_pairs={{1,0},{9,1},{17,2},{25,3},{5,4},{13,5},{21,6},{29,7},{2,8},{10,9},... | collective-permute-start | bytes 1179656 | tf_op jit(solution)/shard_map/ppermute | solution.py:348
  16.3 25.1 %collective-permute-start.10 = (f32[384,256]{1,0:T(8,128)S(1)}, f32[384,256]{1,0:T(8,128)S(1)}, u32[]{:S(2)}, u32[]{:S(2)}) collective-permute-start(f32[384,256]{1,0:T(8,128)S(1)} %get-tuple-element.66), channel_id=1, source_target_pairs={{2,0},{10,1},{18,2},{26,3},{6,4},{14,5},{22,6},{30,7},{3,8},{11,9}... | collective-permute-start | bytes 1179656 | tf_op jit(solution)/shard_map/ppermute | solution.py:348
  17.2 41.7 %collective-permute-start.11 = (f32[384,256]{1,0:T(8,128)S(1)}, f32[384,256]{1,0:T(8,128)S(1)}, u32[]{:S(2)}, u32[]{:S(2)}) collective-permute-start(f32[384,256]{1,0:T(8,128)S(1)} %get-tuple-element.66), channel_id=1, source_target_pairs={{3,0},{11,1},{19,2},{27,3},{7,4},{15,5},{23,6},{31,7},{0,8},{8,9},... | collective-permute-start | bytes 1179656 | tf_op jit(solution)/shard_map/ppermute | solution.py:348
  19.5 41.1 %collective-permute-start = (f32[384,128]{1,0:T(8,128)S(1)}, f32[384,128]{1,0:T(8,128)S(1)}, u32[]{:S(2)}, u32[]{:S(2)}) collective-permute-start(f32[384,128]{1,0:T(8,128)S(1)} %get-tuple-element.63), channel_id=1, source_target_pairs={{0,0},{8,1},{16,2},{24,3},{4,4},{12,5},{20,6},{28,7},{1,8},{9,9},{... | collective-permute-start | bytes 589832 | tf_op jit(solution)/shard_map/ppermute | solution.py:348
  20.1 40.5 %collective-permute-start.1 = (f32[384,128]{1,0:T(8,128)S(1)}, f32[384,128]{1,0:T(8,128)S(1)}, u32[]{:S(2)}, u32[]{:S(2)}) collective-permute-start(f32[384,128]{1,0:T(8,128)S(1)} %get-tuple-element.63), channel_id=1, source_target_pairs={{1,0},{9,1},{17,2},{25,3},{5,4},{13,5},{21,6},{29,7},{2,8},{10,9},... | collective-permute-start | bytes 589832 | tf_op jit(solution)/shard_map/ppermute | solution.py:348
  29.7 32.5 %collective-permute-start.2 = (f32[384,128]{1,0:T(8,128)S(1)}, f32[384,128]{1,0:T(8,128)S(1)}, u32[]{:S(2)}, u32[]{:S(2)}) collective-permute-start(f32[384,128]{1,0:T(8,128)S(1)} %get-tuple-element.63), channel_id=1, source_target_pairs={{2,0},{10,1},{18,2},{26,3},{6,4},{14,5},{22,6},{30,7},{3,8},{11,9}... | collective-permute-start | bytes 589832 | tf_op jit(solution)/shard_map/ppermute | solution.py:348
  41.4 20.8 %collective-permute-start.3 = (f32[384,128]{1,0:T(8,128)S(1)}, f32[384,128]{1,0:T(8,128)S(1)}, u32[]{:S(2)}, u32[]{:S(2)}) collective-permute-start(f32[384,128]{1,0:T(8,128)S(1)} %get-tuple-element.63), channel_id=1, source_target_pairs={{3,0},{11,1},{19,2},{27,3},{7,4},{15,5},{23,6},{31,7},{0,8},{8,9},... | collective-permute-start | bytes 589832 | tf_op jit(solution)/shard_map/ppermute | solution.py:348
  59.0 36.2 %copy-start.3 = (f32[4,384,256]{2,1,0:T(8,128)}, f32[4,384,256]{2,1,0:T(8,128)S(1)}, u32[]{:S(2)}) copy-start(f32[4,384,256]{2,1,0:T(8,128)S(1)} %pad_maximum_fusion.refs_0_) | copy-start | bytes 4718596
  59.0 68.5 %collective-permute-start.12 = (f32[4,384,256]{2,1,0:T(8,128)S(1)}, f32[4,384,256]{2,1,0:T(8,128)}, u32[]{:S(2)}, u32[]{:S(2)}) collective-permute-start(f32[4,384,256]{2,1,0:T(8,128)S(1)} %pad_maximum_fusion.refs_0_), channel_id=1, source_target_pairs={{0,4},{4,0},{1,5},{5,1},{2,6},{6,2},{3,7},{7,3},{8,12},{12,8},{9,1... | collective-permute-start | bytes 4718600 | tf_op jit(solution)/shard_map/ppermute | solution.py:280
  60.6 34.7 %copy-start.18 = (f32[384,128]{1,0:T(8,128)}, f32[384,128]{1,0:T(8,128)S(1)}, u32[]{:S(2)}) copy-start(f32[384,128]{1,0:T(8,128)S(1)} %collective-permute-done) | copy-start | bytes 589828
  60.6 34.6 %copy-start.20 = (f32[384,128]{1,0:T(8,128)}, f32[384,128]{1,0:T(8,128)S(1)}, u32[]{:S(2)}) copy-start(f32[384,128]{1,0:T(8,128)S(1)} %collective-permute-done.1) | copy-start | bytes 589828
  62.2 33.1 %copy-start.22 = (f32[384,128]{1,0:T(8,128)}, f32[384,128]{1,0:T(8,128)S(1)}, u32[]{:S(2)}) copy-start(f32[384,128]{1,0:T(8,128)S(1)} %collective-permute-done.2) | copy-start | bytes 589828
  62.2 33.1 %copy-start.24 = (f32[384,128]{1,0:T(8,128)}, f32[384,128]{1,0:T(8,128)S(1)}, u32[]{:S(2)}) copy-start(f32[384,128]{1,0:T(8,128)S(1)} %collective-permute-done.3) | copy-start | bytes 589828
  62.2 11.8 %collective-permute-start.15 = (f32[384,256]{1,0:T(8,128)S(1)}, f32[384,256]{1,0:T(8,128)S(1)}, u32[]{:S(2)}, u32[]{:S(2)}) collective-permute-start(f32[384,256]{1,0:T(8,128)S(1)} %get-tuple-element.35), channel_id=1, source_target_pairs={{0,0},{8,1},{16,2},{24,3},{4,4},{12,5},{20,6},{28,7},{1,8},{9,9},{... | collective-permute-start | bytes 1179656 | tf_op jit(solution)/shard_map/ppermute | solution.py:348
  62.9 16.4 %collective-permute-start.16 = (f32[384,256]{1,0:T(8,128)S(1)}, f32[384,256]{1,0:T(8,128)S(1)}, u32[]{:S(2)}, u32[]{:S(2)}) collective-permute-start(f32[384,256]{1,0:T(8,128)S(1)} %get-tuple-element.35), channel_id=1, source_target_pairs={{1,0},{9,1},{17,2},{25,3},{5,4},{13,5},{21,6},{29,7},{2,8},{10,9},... | collective-permute-start | bytes 1179656 | tf_op jit(solution)/shard_map/ppermute | solution.py:348
  69.8 19.1 %collective-permute-start.17 = (f32[384,256]{1,0:T(8,128)S(1)}, f32[384,256]{1,0:T(8,128)S(1)}, u32[]{:S(2)}, u32[]{:S(2)}) collective-permute-start(f32[384,256]{1,0:T(8,128)S(1)} %get-tuple-element.35), channel_id=1, source_target_pairs={{2,0},{10,1},{18,2},{26,3},{6,4},{14,5},{22,6},{30,7},{3,8},{11,9}... | collective-permute-start | bytes 1179656 | tf_op jit(solution)/shard_map/ppermute | solution.py:348
  73.8 20.3 %collective-permute-start.18 = (f32[384,256]{1,0:T(8,128)S(1)}, f32[384,256]{1,0:T(8,128)S(1)}, u32[]{:S(2)}, u32[]{:S(2)}) collective-permute-start(f32[384,256]{1,0:T(8,128)S(1)} %get-tuple-element.35), channel_id=1, source_target_pairs={{3,0},{11,1},{19,2},{27,3},{7,4},{15,5},{23,6},{31,7},{0,8},{8,9},... | collective-permute-start | bytes 1179656 | tf_op jit(solution)/shard_map/ppermute | solution.py:348
  95.3 43.3 %collective-permute-start.19 = (f32[4,384,256]{2,1,0:T(8,128)}, f32[4,384,256]{2,1,0:T(8,128)}, u32[]{:S(2)}, u32[]{:S(2)}) collective-permute-start(f32[4,384,256]{2,1,0:T(8,128)} %pad_maximum_fusion.1.refs_0_), channel_id=1, source_target_pairs={{0,4},{4,0},{1,5},{5,1},{2,6},{6,2},{3,7},{7,3},{8,12},{12,8},{9,1... | collective-permute-start | bytes 4718600 | tf_op jit(solution)/shard_map/ppermute | solution.py:280
  96.8 52.8 %collective-permute-start.6 = (f32[384,1024]{1,0:T(8,128)S(1)}, f32[384,1024]{1,0:T(8,128)}, u32[]{:S(2)}, u32[]{:S(2)}) collective-permute-start(f32[384,1024]{1,0:T(8,128)S(1)} %copy-done), channel_id=1, source_target_pairs={{0,2},{2,0},{1,3},{3,1},{4,6},{6,4},{5,7},{7,5},{8,10},{10,8},{9,1... | collective-permute-start | bytes 4718600 | tf_op jit(solution)/shard_map/ppermute | solution.py:280
  138.5 15.5 %collective-permute-start.13 = (f32[2,384,256]{2,1,0:T(8,128)}, f32[2,384,256]{2,1,0:T(8,128)S(1)}, u32[]{:S(2)}, u32[]{:S(2)}) collective-permute-start(f32[2,384,256]{2,1,0:T(8,128)} %get-tuple-element.33), channel_id=1, source_target_pairs={{0,1},{1,0},{2,3},{3,2},{4,5},{5,4},{6,7},{7,6},{8,9},{9,8},{10,11... | collective-permute-start | bytes 2359304 | tf_op jit(solution)/shard_map/ppermute | solution.py:280
  149.5 11.5 %collective-permute-start.20 = (f32[2,384,256]{2,1,0:T(8,128)}, f32[2,384,256]{2,1,0:T(8,128)S(1)}, u32[]{:S(2)}, u32[]{:S(2)}) collective-permute-start(f32[2,384,256]{2,1,0:T(8,128)} %get-tuple-element.37), channel_id=1, source_target_pairs={{0,1},{1,0},{2,3},{3,2},{4,5},{5,4},{6,7},{7,6},{8,9},{9,8},{10,11... | collective-permute-start | bytes 2359304 | tf_op jit(solution)/shard_map/ppermute | solution.py:280
  168.0 45.1 %collective-permute-start.29 = (f32[512,512]{1,0:T(8,128)S(1)}, f32[512,512]{1,0:T(8,128)S(1)}, u32[]{:S(2)}, u32[]{:S(2)}) collective-permute-start(f32[512,512]{1,0:T(8,128)S(1)} %pad_maximum_fusion.3), channel_id=1, source_target_pairs={{0,1},{1,0},{2,3},{3,2},{4,5},{5,4},{6,7},{7,6},{8,9},{9,8},{10,11... | collective-permute-start | bytes 3145736 | tf_op jit(solution)/shard_map/ppermute | solution.py:280
  168.6 22.4 %collective-permute-start.22 = (f32[384,256]{1,0:T(8,128)S(1)}, f32[384,256]{1,0:T(8,128)S(1)}, u32[]{:S(2)}, u32[]{:S(2)}) collective-permute-start(f32[384,256]{1,0:T(8,128)S(1)} %get-tuple-element.39), channel_id=1, source_target_pairs={{0,0},{8,1},{16,2},{24,3},{4,4},{12,5},{20,6},{28,7},{1,8},{9,9},{... | collective-permute-start | bytes 1179656 | tf_op jit(solution)/shard_map/ppermute | solution.py:348
  169.3 21.7 %collective-permute-start.23 = (f32[384,256]{1,0:T(8,128)S(1)}, f32[384,256]{1,0:T(8,128)S(1)}, u32[]{:S(2)}, u32[]{:S(2)}) collective-permute-start(f32[384,256]{1,0:T(8,128)S(1)} %get-tuple-element.39), channel_id=1, source_target_pairs={{1,0},{9,1},{17,2},{25,3},{5,4},{13,5},{21,6},{29,7},{2,8},{10,9},... | collective-permute-start | bytes 1179656 | tf_op jit(solution)/shard_map/ppermute | solution.py:348
  175.3 31.0 %collective-permute-start.24 = (f32[384,256]{1,0:T(8,128)S(1)}, f32[384,256]{1,0:T(8,128)S(1)}, u32[]{:S(2)}, u32[]{:S(2)}) collective-permute-start(f32[384,256]{1,0:T(8,128)S(1)} %get-tuple-element.39), channel_id=1, source_target_pairs={{2,0},{10,1},{18,2},{26,3},{6,4},{14,5},{22,6},{30,7},{3,8},{11,9}... | collective-permute-start | bytes 1179656 | tf_op jit(solution)/shard_map/ppermute | solution.py:348
  187.0 19.3 %collective-permute-start.25 = (f32[384,256]{1,0:T(8,128)S(1)}, f32[384,256]{1,0:T(8,128)S(1)}, u32[]{:S(2)}, u32[]{:S(2)}) collective-permute-start(f32[384,256]{1,0:T(8,128)S(1)} %get-tuple-element.39), channel_id=1, source_target_pairs={{3,0},{11,1},{19,2},{27,3},{7,4},{15,5},{23,6},{31,7},{0,8},{8,9},... | collective-permute-start | bytes 1179656 | tf_op jit(solution)/shard_map/ppermute | solution.py:348
  206.4 7.9 %copy-start.4 = (f32[4,384,256]{2,1,0:T(8,128)}, f32[4,384,256]{2,1,0:T(8,128)S(1)}, u32[]{:S(2)}) copy-start(f32[4,384,256]{2,1,0:T(8,128)S(1)} %pad_maximum_fusion.2.refs_0_) | copy-start | bytes 4718596
  206.4 46.6 %collective-permute-start.26 = (f32[4,384,256]{2,1,0:T(8,128)S(1)}, f32[4,384,256]{2,1,0:T(8,128)}, u32[]{:S(2)}, u32[]{:S(2)}) collective-permute-start(f32[4,384,256]{2,1,0:T(8,128)S(1)} %pad_maximum_fusion.2.refs_0_), channel_id=1, source_target_pairs={{0,4},{4,0},{1,5},{5,1},{2,6},{6,2},{3,7},{7,3},{8,12},{12,8},{9,1... | collective-permute-start | bytes 4718600 | tf_op jit(solution)/shard_map/ppermute | solution.py:280
  214.3 49.7 %all-to-all-start = ((f32[16,32,512]{2,1,0:T(8,128)}), f32[16,32,512]{2,1,0:T(8,128)S(1)}, u32[]{:S(2)}, u32[]{:S(2)}) async-start(f32[16,32,512]{2,1,0:T(8,128)} %bitcast.33), calls=%async_computation | async-start | bytes 2097152 | tf_op jit(solution)/shard_map/all_to_all | solution.py:384
  264.1 19.4 %copy-start.26 = (f32[384,128]{1,0:T(8,128)S(1)}, f32[384,128]{1,0:T(8,128)}, u32[]{:S(2)}) copy-start(f32[384,128]{1,0:T(8,128)} %get-tuple-element.47) | copy-start | bytes 589828
  265.2 84.0 %all-to-all-start.1 = ((f32[16,32,512]{2,1,0:T(8,128)}), f32[16,32,512]{2,1,0:T(8,128)S(1)}, u32[]{:S(2)}, u32[]{:S(2)}) async-start(f32[16,32,512]{2,1,0:T(8,128)} %broadcast_in_dim.33), calls=%async_computation.1 | async-start | bytes 2097152 | tf_op jit(solution)/shard_map/all_to_all | solution.py:289
  283.4 9.8 %collective-permute-start.30 = (f32[384,128]{1,0:T(8,128)S(1)}, f32[384,128]{1,0:T(8,128)S(1)}, u32[]{:S(2)}, u32[]{:S(2)}) collective-permute-start(f32[384,128]{1,0:T(8,128)S(1)} %copy-done.26), channel_id=1, source_target_pairs={{0,0},{8,1},{16,2},{24,3},{4,4},{12,5},{20,6},{28,7},{1,8},{9,9},{... | collective-permute-start | bytes 589832 | tf_op jit(solution)/shard_map/ppermute | solution.py:348
  284.1 19.5 %collective-permute-start.31 = (f32[384,128]{1,0:T(8,128)S(1)}, f32[384,128]{1,0:T(8,128)S(1)}, u32[]{:S(2)}, u32[]{:S(2)}) collective-permute-start(f32[384,128]{1,0:T(8,128)S(1)} %copy-done.26), channel_id=1, source_target_pairs={{1,0},{9,1},{17,2},{25,3},{5,4},{13,5},{21,6},{29,7},{2,8},{10,9},... | collective-permute-start | bytes 589832 | tf_op jit(solution)/shard_map/ppermute | solution.py:348
  292.7 18.9 %collective-permute-start.32 = (f32[384,128]{1,0:T(8,128)S(1)}, f32[384,128]{1,0:T(8,128)S(1)}, u32[]{:S(2)}, u32[]{:S(2)}) collective-permute-start(f32[384,128]{1,0:T(8,128)S(1)} %copy-done.26), channel_id=1, source_target_pairs={{2,0},{10,1},{18,2},{26,3},{6,4},{14,5},{22,6},{30,7},{3,8},{11,9}... | collective-permute-start | bytes 589832 | tf_op jit(solution)/shard_map/ppermute | solution.py:348
  293.3 18.8 %collective-permute-start.33 = (f32[384,128]{1,0:T(8,128)S(1)}, f32[384,128]{1,0:T(8,128)S(1)}, u32[]{:S(2)}, u32[]{:S(2)}) collective-permute-start(f32[384,128]{1,0:T(8,128)S(1)} %copy-done.26), channel_id=1, source_target_pairs={{3,0},{11,1},{19,2},{27,3},{7,4},{15,5},{23,6},{31,7},{0,8},{8,9},... | collective-permute-start | bytes 589832 | tf_op jit(solution)/shard_map/ppermute | solution.py:348
  312.1 19.9 %copy-start.1 = (f32[4,384,128]{2,1,0:T(8,128)}, f32[4,384,128]{2,1,0:T(8,128)S(1)}, u32[]{:S(2)}) copy-start(f32[4,384,128]{2,1,0:T(8,128)S(1)} %pad_maximum_fusion.5.refs_0_) | copy-start | bytes 2359300
  312.1 19.9 %collective-permute-start.34 = (f32[4,384,128]{2,1,0:T(8,128)S(1)}, f32[4,384,128]{2,1,0:T(8,128)S(1)}, u32[]{:S(2)}, u32[]{:S(2)}) collective-permute-start(f32[4,384,128]{2,1,0:T(8,128)S(1)} %pad_maximum_fusion.5.refs_0_), channel_id=1, source_target_pairs={{0,4},{4,0},{1,5},{5,1},{2,6},{6,2},{3,7},{7,3},{8,12},{12,8},{9,1... | collective-permute-start | bytes 2359304 | tf_op jit(solution)/shard_map/ppermute | solution.py:280
  314.5 27.7 %collective-permute-start.27 = (f32[2,384,256]{2,1,0:T(8,128)}, f32[2,384,256]{2,1,0:T(8,128)S(1)}, u32[]{:S(2)}, u32[]{:S(2)}) collective-permute-start(f32[2,384,256]{2,1,0:T(8,128)} %get-tuple-element.41), channel_id=1, source_target_pairs={{0,1},{1,0},{2,3},{3,2},{4,5},{5,4},{6,7},{7,6},{8,9},{9,8},{10,11... | collective-permute-start | bytes 2359304 | tf_op jit(solution)/shard_map/ppermute | solution.py:280
  341.8 7.4 %collective-permute-start.35 = (f32[2,384,128]{2,1,0:T(8,128)}, f32[2,384,128]{2,1,0:T(8,128)S(1)}, u32[]{:S(2)}, u32[]{:S(2)}) collective-permute-start(f32[2,384,128]{2,1,0:T(8,128)} %get-tuple-element.51), channel_id=1, source_target_pairs={{0,1},{1,0},{2,3},{3,2},{4,5},{5,4},{6,7},{7,6},{8,9},{9,8},{10,11... | collective-permute-start | bytes 1179656 | tf_op jit(solution)/shard_map/ppermute | solution.py:280
  355.4 2.4 collective-permute-start.38
  357.8 22.4 %copy-start.19 = (f32[384,128]{1,0:T(8,128)S(1)}, f32[384,128]{1,0:T(8,128)}, u32[]{:S(2)}) copy-start(f32[384,128]{1,0:T(8,128)} %copy-done.18) | copy-start | bytes 589828
  357.8 22.4 %copy-start.21 = (f32[384,128]{1,0:T(8,128)S(1)}, f32[384,128]{1,0:T(8,128)}, u32[]{:S(2)}) copy-start(f32[384,128]{1,0:T(8,128)} %copy-done.20) | copy-start | bytes 589828
  357.8 22.4 %copy-start.23 = (f32[384,128]{1,0:T(8,128)S(1)}, f32[384,128]{1,0:T(8,128)}, u32[]{:S(2)}) copy-start(f32[384,128]{1,0:T(8,128)} %copy-done.22) | copy-start | bytes 589828
  357.8 22.4 %copy-start.25 = (f32[384,128]{1,0:T(8,128)S(1)}, f32[384,128]{1,0:T(8,128)}, u32[]{:S(2)}) copy-start(f32[384,128]{1,0:T(8,128)} %copy-done.24) | copy-start | bytes 589828
  358.8 59.0 %all-to-all-start.2 = ((f32[16,32,384]{2,1,0:T(8,128)}), f32[16,32,384]{2,1,0:T(8,128)S(1)}, u32[]{:S(2)}, u32[]{:S(2)}) async-start(f32[16,32,384]{2,1,0:T(8,128)} %bitcast.46), calls=%async_computation.2 | async-start | bytes 1572864 | tf_op jit(solution)/shard_map/all_to_all | solution.py:384
  380.2 27.7 %copy-start.2 = (f32[4,384,128]{2,1,0:T(8,128)}, f32[4,384,128]{2,1,0:T(8,128)S(1)}, u32[]{:S(2)}) copy-start(f32[4,384,128]{2,1,0:T(8,128)S(1)} %pad_maximum_fusion.4.refs_0_) | copy-start | bytes 2359300
  380.3 27.7 %collective-permute-start.4 = (f32[4,384,128]{2,1,0:T(8,128)S(1)}, f32[4,384,128]{2,1,0:T(8,128)S(1)}, u32[]{:S(2)}, u32[]{:S(2)}) collective-permute-start(f32[4,384,128]{2,1,0:T(8,128)S(1)} %pad_maximum_fusion.4.refs_0_), channel_id=1, source_target_pairs={{0,4},{4,0},{1,5},{5,1},{2,6},{6,2},{3,7},{7,3},{8,12},{12,8},{9,1... | collective-permute-start | bytes 2359304 | tf_op jit(solution)/shard_map/ppermute | solution.py:280
  417.7 10.9 %collective-permute-start.5 = (f32[2,384,128]{2,1,0:T(8,128)}, f32[2,384,128]{2,1,0:T(8,128)S(1)}, u32[]{:S(2)}, u32[]{:S(2)}) collective-permute-start(f32[2,384,128]{2,1,0:T(8,128)} %get-tuple-element.30), channel_id=1, source_target_pairs={{0,1},{1,0},{2,3},{3,2},{4,5},{5,4},{6,7},{7,6},{8,9},{9,8},{10,11... | collective-permute-start | bytes 1179656 | tf_op jit(solution)/shard_map/ppermute | solution.py:280
  418.8 49.3 %all-to-all-start.3 = ((f32[16,32,384]{2,1,0:T(8,128)}), f32[16,32,384]{2,1,0:T(8,128)}, u32[]{:S(2)}, u32[]{:S(2)}) async-start(f32[16,32,384]{2,1,0:T(8,128)} %broadcast_in_dim.34), calls=%async_computation.3 | async-start | bytes 1572864 | tf_op jit(solution)/shard_map/all_to_all | solution.py:289
  428.6 138.5 %all-reduce.2.cloned.1.call-start = ((), (), s32[]{:S(2)}) async-start(), calls=%async_computation.4 | async-start | bytes 1048576 | tf_op jit(solution)/shard_map/psum | solution.py:378
  429.4 7.5 %copy-start.10 = (f32[2,384,256]{2,1,0:T(8,128)S(1)}, f32[2,384,256]{2,1,0:T(8,128)}, u32[]{:S(2)}) copy-start(f32[2,384,256]{2,1,0:T(8,128)} %get-tuple-element.34) | copy-start | bytes 2359300
  433.8 14.5 %copy-start.12 = (f32[2,384,256]{2,1,0:T(8,128)S(1)}, f32[2,384,256]{2,1,0:T(8,128)}, u32[]{:S(2)}) copy-start(f32[2,384,256]{2,1,0:T(8,128)} %get-tuple-element.42) | copy-start | bytes 2359300
  433.8 14.4 %copy-start.17 = (f32[2,384,128]{2,1,0:T(8,128)S(1)}, f32[2,384,128]{2,1,0:T(8,128)}, u32[]{:S(2)}) copy-start(f32[2,384,128]{2,1,0:T(8,128)} %get-tuple-element.31) | copy-start | bytes 1179652
  434.9 13.3 %collective-permute-start.7 = (f32[384,128]{1,0:T(8,128)S(1)}, f32[384,128]{1,0:T(8,128)S(1)}, u32[]{:S(2)}, u32[]{:S(2)}) collective-permute-start(f32[384,128]{1,0:T(8,128)S(1)} %dynamic-slice_bitcast_fusion.4), channel_id=1, source_target_pairs={{0,2},{2,0},{1,3},{3,1},{4,6},{6,4},{5,7},{7,5},{8,10},{10,8},{9,1... | collective-permute-start | bytes 589832 | tf_op jit(solution)/shard_map/ppermute | solution.py:280
  436.9 20.6 %collective-permute-start.14 = (f32[384,256]{1,0:T(8,128)S(1)}, f32[384,256]{1,0:T(8,128)S(1)}, u32[]{:S(2)}, u32[]{:S(2)}) collective-permute-start(f32[384,256]{1,0:T(8,128)S(1)} %dynamic-slice_bitcast_fusion.2), channel_id=1, source_target_pairs={{0,2},{2,0},{1,3},{3,1},{4,6},{6,4},{5,7},{7,5},{8,10},{10,8},{9,1... | collective-permute-start | bytes 1179656 | tf_op jit(solution)/shard_map/ppermute | solution.py:280
  437.1 28.8 %collective-permute-start.21 = (f32[384,256]{1,0:T(8,128)S(1)}, f32[384,256]{1,0:T(8,128)S(1)}, u32[]{:S(2)}, u32[]{:S(2)}) collective-permute-start(f32[384,256]{1,0:T(8,128)S(1)} %dynamic-slice_bitcast_fusion.1), channel_id=1, source_target_pairs={{0,2},{2,0},{1,3},{3,1},{4,6},{6,4},{5,7},{7,5},{8,10},{10,8},{9,1... | collective-permute-start | bytes 1179656 | tf_op jit(solution)/shard_map/ppermute | solution.py:280
  448.3 17.7 %copy-start.15 = (f32[2,384,128]{2,1,0:T(8,128)S(1)}, f32[2,384,128]{2,1,0:T(8,128)}, u32[]{:S(2)}) copy-start(f32[2,384,128]{2,1,0:T(8,128)} %get-tuple-element.52) | copy-start | bytes 1179652
  449.1 25.7 %collective-permute-start.28 = (f32[384,256]{1,0:T(8,128)}, f32[384,256]{1,0:T(8,128)}, u32[]{:S(2)}, u32[]{:S(2)}) collective-permute-start(f32[384,256]{1,0:T(8,128)} %dynamic-slice_bitcast_fusion), channel_id=1, source_target_pairs={{0,2},{2,0},{1,3},{3,1},{4,6},{6,4},{5,7},{7,5},{8,10},{10,8},{9,1... | collective-permute-start | bytes 1179656 | tf_op jit(solution)/shard_map/ppermute | solution.py:280
  450.5 28.3 %collective-permute-start.37 = (f32[512,512]{1,0:T(8,128)S(1)}, f32[512,512]{1,0:T(8,128)}, u32[]{:S(2)}, u32[]{:S(2)}) collective-permute-start(f32[512,512]{1,0:T(8,128)S(1)} %bitcast.90), channel_id=1, source_target_pairs={{0,1},{1,0},{2,3},{3,2},{4,5},{5,4},{6,7},{7,6},{8,9},{9,8},{10,11... | collective-permute-start | bytes 3145736 | tf_op jit(solution)/shard_map/ppermute | solution.py:280
  457.5 20.6 %copy-start.16 = (f32[2,384,128]{2,1,0:T(8,128)S(1)}, f32[2,384,128]{2,1,0:T(8,128)}, u32[]{:S(2)}) copy-start(f32[2,384,128]{2,1,0:T(8,128)} %get-tuple-element.52) | copy-start | bytes 1179652
  467.1 11.1 %collective-permute-start.36 = (f32[384,128]{1,0:T(8,128)S(1)}, f32[384,128]{1,0:T(8,128)S(1)}, u32[]{:S(2)}, u32[]{:S(2)}) collective-permute-start(f32[384,128]{1,0:T(8,128)S(1)} %dynamic-slice_bitcast_fusion.3), channel_id=1, source_target_pairs={{0,2},{2,0},{1,3},{3,1},{4,6},{6,4},{5,7},{7,5},{8,10},{10,8},{9,1... | collective-permute-start | bytes 589832 | tf_op jit(solution)/shard_map/ppermute | solution.py:280
  468.1 12.3 %collective-permute-start.39 = (f32[512,384]{1,0:T(8,128)}, f32[512,384]{1,0:T(8,128)S(1)}, u32[]{:S(2)}, u32[]{:S(2)}) collective-permute-start(f32[512,384]{1,0:T(8,128)} %bitcast.47), channel_id=1, source_target_pairs={{0,1},{1,0},{2,3},{3,2},{4,5},{5,4},{6,7},{7,6},{8,9},{9,8},{10,11... | collective-permute-start | bytes 2359304 | tf_op jit(solution)/shard_map/ppermute | solution.py:280
  (9 other events, 10.4 us)
Sparse Core Ops, SparseCore 0:
  434.6 132.3 all-reduce.1

commit v2 on v1

--- a/solution.py
+++ b/solution.py
@@ -351,7 +351,9 @@
         theirs = swap(mine, "x")
         parts = (mine, theirs) if ratio == 2 else (jnp.where(column % 2 == x, mine, theirs),)
         gate = after(place, pieces[chunk - 2]) if chunk - 2 in pieces else place
-        kept, send = tile_products(tiles, count, gate, halved, parts, inverse.shape[0], tile_cols)
+        kept, send = tile_products(
+            tiles, count, gate, halved, parts, inverse.shape[0], tile_cols
+        )
         for index, (born, state, value) in list(pending.items()):
             value = after(value, kept)
             if state == 0:
@@ -387,8 +389,16 @@
         if state == 0:
             value = spread(jnp.sum(value, axis=0), CHIPS)
         diags[index] = assemble(value, width, k)
-    diags = [piece for index in sorted(diags) for piece in diags[index]]
-    return jnp.concatenate(panels, 1), diag_inverse + jnp.concatenate(diags, 1)
+    starts = [sum(shares(width)[:chunk]) * LANES for chunk in range(len(panels) + 1)]
+    total = diag_inverse
+    for index in sorted(diags, key=lambda index: 1.5 if index in OFFLOADED else index):
+        pieces = diags[index]
+        members = groups[index]
+        for piece, chunk in zip(pieces, members if index in OFFLOADED else members[:1]):
+            first = starts[chunk]
+            columns = total[:, first : first + piece.shape[1]] + piece
+            total = lax.dynamic_update_slice(total, columns, (0, first))
+    return jnp.concatenate(panels, 1), total
 
 
 def assemble(value, width, k):

time: 581 us -> 575 us (0.990)
  waiting for transfers between devices: 240 us -> 209 us
  starting transfers between devices: 198 us -> 217 us
    ppermute x20, waiting for transfers between devices: 100 us -> 62 us  [swap(): return lax.ppermute(value, axis, [(0, 1), (1, 0)])]
    all_to_all x2, starting transfers between devices: 27.9 us -> 41.9 us  [spread(): return lax.all_to_all(copies, axes, split_axis=0, concat_axis=0)]
    dynamic_update_slice x0 -> x3, other arithmetic: none -> 8.22 us  [step_body(): total = lax.dynamic_update_slice(total, columns, (0, first))]
  transfers between devices with their start and end apart: 45 -> 45, of which waited for: 18 -> 20; matrix products, arithmetic and copies ran while one was open for 4% -> 5% of each run, Pallas kernels for 13% -> 14%
where the time goes in v2:
time: 575 us; the launch traced here: 574 us
  starting transfers between devices  217 us (38%)
  waiting for transfers between devices  209 us (36%)
  Pallas kernels  86.9 us (15%)
  other arithmetic  23.8 us (4%)
  local copies, waits for them, and re-layouts  22.7 us (4%)
  between operations  14.6 us (3%)
    ppermute x20, starting transfers between devices, step_body(): mine.append(lax.ppermute(part, DEVICES, routes(planes, cols, j)))  90.4 us
    psum x1, waiting for transfers between devices, step_body(): diags[index] = lax.psum([term.reshape(width, -1) for term in mine], DEVICES)  87.7 us
    ppermute x20, waiting for transfers between devices, swap(): return lax.ppermute(value, axis, [(0, 1), (1, 0)])  62 us
    ppermute x20, waiting for transfers between devices, step_body(): mine.append(lax.ppermute(part, DEVICES, routes(planes, cols, j)))  57.9 us
    pallas_call x5, Pallas kernels, tile_products(): pl.pallas_call(functools.partial(tiles_kernel, tile_cols, len(parts)), ou...  50.7 us
    ppermute x20, starting transfers between devices, swap(): return lax.ppermute(value, axis, [(0, 1), (1, 0)])  44.1 us
    all_to_all x2, starting transfers between devices, spread(): return lax.all_to_all(copies, axes, split_axis=0, concat_axis=0)  41.9 us
    all_to_all x2, starting transfers between devices, step_body(): value = lax.all_to_all(sent, CHIPS, split_axis=0, concat_axis=0)  40.1 us
  transfers between devices with their start and end apart: 45, of which 20 were waited for; matrix products, arithmetic and copies ran while one was open for 5% of the time, Pallas kernels for 14%

profile of v2, /device:TPU:0, one launch (start us, length us, event | category | flops | bytes accessed | tf_op | source)
XLA Modules:
  0.0 574.1 jit_solution(12573927874414066933)
XLA Ops:
  7.2 4.9 copy.18
  12.2 3.1 collective-permute-start.11
  15.3 2.4 collective-permute-start.10
  20.2 2.3 collective-permute-start.3
  22.5 1.9 collective-permute-done.11
  24.4 8.2 %collective-permute-start.2 = (f32[384,128]{1,0:T(8,128)S(1)}, f32[384,128]{1,0:T(8,128)S(1)}, u32[]{:S(2)}, u32[]{:S(2)}) collective-permute-start(f32[384,128]{1,0:T(8,128)S(1)} %get-tuple-element.63), channel_id=1, source_target_pairs={{2,0},{10,1},{18,2},{26,3},{6,4},{14,5},{22,6},{30,7},{3,8},{11,9}... | collective-permute-start | bytes 589832 | tf_op jit(solution)/shard_map/ppermute | solution.py:348
  32.8 11.3 %collective-permute-start.1 = (f32[384,128]{1,0:T(8,128)S(1)}, f32[384,128]{1,0:T(8,128)S(1)}, u32[]{:S(2)}, u32[]{:S(2)}) collective-permute-start(f32[384,128]{1,0:T(8,128)S(1)} %get-tuple-element.63), channel_id=1, source_target_pairs={{1,0},{9,1},{17,2},{25,3},{5,4},{13,5},{21,6},{29,7},{2,8},{10,9},... | collective-permute-start | bytes 589832 | tf_op jit(solution)/shard_map/ppermute | solution.py:348
  45.0 1.4 collective-permute-start.12
  46.4 3.3 collective-permute-done.2
  49.7 2.5 collective-permute-done.1
  52.3 15.8 %collective-permute-start.18 = (f32[384,256]{1,0:T(8,128)S(1)}, f32[384,256]{1,0:T(8,128)S(1)}, u32[]{:S(2)}, u32[]{:S(2)}) collective-permute-start(f32[384,256]{1,0:T(8,128)S(1)} %get-tuple-element.35), channel_id=1, source_target_pairs={{3,0},{11,1},{19,2},{27,3},{7,4},{15,5},{23,6},{31,7},{0,8},{8,9},... | collective-permute-start | bytes 1179656 | tf_op jit(solution)/shard_map/ppermute | solution.py:348
  68.1 20.1 %collective-permute-start.17 = (f32[384,256]{1,0:T(8,128)S(1)}, f32[384,256]{1,0:T(8,128)S(1)}, u32[]{:S(2)}, u32[]{:S(2)}) collective-permute-start(f32[384,256]{1,0:T(8,128)S(1)} %get-tuple-element.35), channel_id=1, source_target_pairs={{2,0},{10,1},{18,2},{26,3},{6,4},{14,5},{22,6},{30,7},{3,8},{11,9}... | collective-permute-start | bytes 1179656 | tf_op jit(solution)/shard_map/ppermute | solution.py:348
  88.9 7.2 %collective-permute-done.17 = f32[384,256]{1,0:T(8,128)S(1)} collective-permute-done((f32[384,256]{1,0:T(8,128)S(1)}, f32[384,256]{1,0:T(8,128)S(1)}, u32[]{:S(2)}, u32[]{:S(2)}) %collective-permute-start.17) | collective-permute-done | bytes 393248 | tf_op jit(solution)/shard_map/ppermute | solution.py:348
  96.1 5.9 %collective-permute-done.16 = f32[384,256]{1,0:T(8,128)S(1)} collective-permute-done((f32[384,256]{1,0:T(8,128)S(1)}, f32[384,256]{1,0:T(8,128)S(1)}, u32[]{:S(2)}, u32[]{:S(2)}) %collective-permute-start.16) | collective-permute-done | bytes 393248 | tf_op jit(solution)/shard_map/ppermute | solution.py:348
  102.0 1.3 pad_maximum_fusion.1.refs_0_
  103.3 1.6 collective-permute-start.19
  104.8 16.3 %collective-permute-start.6 = (f32[384,1024]{1,0:T(8,128)S(1)}, f32[384,1024]{1,0:T(8,128)}, u32[]{:S(2)}, u32[]{:S(2)}) collective-permute-start(f32[384,1024]{1,0:T(8,128)S(1)} %copy-done), channel_id=1, source_target_pairs={{0,2},{2,0},{1,3},{3,1},{4,6},{6,4},{5,7},{7,5},{8,10},{10,8},{9,1... | collective-permute-start | bytes 4718600 | tf_op jit(solution)/shard_map/ppermute | solution.py:280
  121.1 1.5 fusion.14
  126.0 8.8 %halve.1.parts_ref = bf16[18,512,1024]{2,1,0:T(8,128)(2,1)} custom-call(s32[18]{0:T(128)} %select_reduce_fusion.tiles_ref, s32[1]{0:T(128)} %bitcast.4.count_ref, f32[1536,3072]{1,0:T(8,128)} %inverse_ref.1), custom_call_target="tpu_custom_call" | custom-call | bytes 37748736 | tf_op jit(solution)/shard_map/halve/pallas_call | solution.py:87
  135.4 10.9 %tiles.6 = (f32[2,384,256]{2,1,0:T(8,128)}, f32[2,384,256]{2,1,0:T(8,128)}) custom-call(s32[18]{0:T(128)} %select_reduce_fusion.tiles_ref, s32[1]{0:T(128)} %bitcast.4.count_ref, s32[4]{0:T(128)} %pad_add_fusion.place_ref, bf16[18,512,1024]{2,1,0:T(8,128)(2,1)} %halve.1.parts_ref, f32[4,384,256]{2,1,0:T(8,128)} %copy-done.3, ...), custom_call_target="tpu_custom_call" | custom-call | flops 7247757312 | bytes 18874368 | tf_op jit(solution)/shard_map/tiles/pallas_call | solution.py:185
  146.4 10.9 %tiles.7 = (f32[2,384,256]{2,1,0:T(8,128)}, f32[2,384,256]{2,1,0:T(8,128)}) custom-call(s32[18]{0:T(128)} %select_reduce_fusion.tiles_ref, s32[1]{0:T(128)} %bitcast.4.count_ref, s32[4]{0:T(128)} %pad_add_fusion.place_ref, bf16[18,512,1024]{2,1,0:T(8,128)(2,1)} %halve.1.parts_ref, f32[4,384,256]{2,1,0:T(8,128)} %pad_maximum_fusion.1.refs_0_, ...), custom_call_target="tpu_custom_call" | custom-call | flops 7247757312 | bytes 18874368 | tf_op jit(solution)/shard_map/tiles/pallas_call | solution.py:185
  157.5 4.4 turn.1.turned_ref
  162.8 4.7 finish.6
  167.5 1.3 slice_bitcast_fusion.5
  169.7 4.7 finish.7
  174.5 1.3 slice_bitcast_fusion.4
  176.4 17.3 %collective-permute-start.24 = (f32[384,256]{1,0:T(8,128)S(1)}, f32[384,256]{1,0:T(8,128)S(1)}, u32[]{:S(2)}, u32[]{:S(2)}) collective-permute-start(f32[384,256]{1,0:T(8,128)S(1)} %get-tuple-element.39), channel_id=1, source_target_pairs={{2,0},{10,1},{18,2},{26,3},{6,4},{14,5},{22,6},{30,7},{3,8},{11,9}... | collective-permute-start | bytes 1179656 | tf_op jit(solution)/shard_map/ppermute | solution.py:348
  194.4 8.9 %collective-permute-done.24 = f32[384,256]{1,0:T(8,128)S(1)} collective-permute-done((f32[384,256]{1,0:T(8,128)S(1)}, f32[384,256]{1,0:T(8,128)S(1)}, u32[]{:S(2)}, u32[]{:S(2)}) %collective-permute-start.24) | collective-permute-done | bytes 393248 | tf_op jit(solution)/shard_map/ppermute | solution.py:348
  203.2 8.5 %collective-permute-done.23 = f32[384,256]{1,0:T(8,128)S(1)} collective-permute-done((f32[384,256]{1,0:T(8,128)S(1)}, f32[384,256]{1,0:T(8,128)S(1)}, u32[]{:S(2)}, u32[]{:S(2)}) %collective-permute-start.23) | collective-permute-done | bytes 393248 | tf_op jit(solution)/shard_map/ppermute | solution.py:348
  211.8 3.9 collective-permute-start.26
  217.0 17.3 %all-to-all-start = ((f32[16,32,512]{2,1,0:T(8,128)}), f32[16,32,512]{2,1,0:T(8,128)S(1)}, u32[]{:S(2)}, u32[]{:S(2)}) async-start(f32[16,32,512]{2,1,0:T(8,128)} %bitcast.33), calls=%async_computation | async-start | bytes 2097152 | tf_op jit(solution)/shard_map/all_to_all | solution.py:386
  234.3 21.2 %collective-permute-done.26.refs_1_ = f32[4,384,256]{2,1,0:T(8,128)} collective-permute-done((f32[4,384,256]{2,1,0:T(8,128)S(1)}, f32[4,384,256]{2,1,0:T(8,128)}, u32[]{:S(2)}, u32[]{:S(2)}) %collective-permute-start.26) | collective-permute-done | bytes 1572896 | tf_op jit(solution)/shard_map/ppermute | solution.py:280
  255.5 10.9 %tiles.8 = (f32[2,384,256]{2,1,0:T(8,128)}, f32[2,384,256]{2,1,0:T(8,128)}) custom-call(s32[18]{0:T(128)} %select_reduce_fusion.tiles_ref, s32[1]{0:T(128)} %bitcast.4.count_ref, s32[4]{0:T(128)} %pad_add_fusion.place_ref, bf16[18,512,1024]{2,1,0:T(8,128)(2,1)} %halve.1.parts_ref, f32[4,384,256]{2,1,0:T(8,128)} %copy-done.4, ...), custom_call_target="tpu_custom_call" | custom-call | flops 7247757312 | bytes 18874368 | tf_op jit(solution)/shard_map/tiles/pallas_call | solution.py:185
  266.4 1.8 all-to-all-done
  269.5 26.1 %all-to-all-start.1 = ((f32[16,32,512]{2,1,0:T(8,128)}), f32[16,32,512]{2,1,0:T(8,128)S(1)}, u32[]{:S(2)}, u32[]{:S(2)}) async-start(f32[16,32,512]{2,1,0:T(8,128)} %broadcast_in_dim.33), calls=%async_computation.1 | async-start | bytes 2097152 | tf_op jit(solution)/shard_map/all_to_all | solution.py:289
  295.6 2.0 collective-permute-start.33
  297.6 2.4 collective-permute-start.32
  301.8 15.1 %collective-permute-done.33 = f32[384,128]{1,0:T(8,128)S(1)} collective-permute-done((f32[384,128]{1,0:T(8,128)S(1)}, f32[384,128]{1,0:T(8,128)S(1)}, u32[]{:S(2)}, u32[]{:S(2)}) %collective-permute-start.33) | collective-permute-done | bytes 196640 | tf_op jit(solution)/shard_map/ppermute | solution.py:348
  316.9 2.1 collective-permute-done.32
  319.1 2.1 collective-permute-done.31
  321.2 1.8 collective-permute-start.34
  323.0 13.5 %collective-permute-done.34.refs_1_ = f32[4,384,128]{2,1,0:T(8,128)S(1)} collective-permute-done((f32[4,384,128]{2,1,0:T(8,128)S(1)}, f32[4,384,128]{2,1,0:T(8,128)S(1)}, u32[]{:S(2)}, u32[]{:S(2)}) %collective-permute-start.34) | collective-permute-done | bytes 786464 | tf_op jit(solution)/shard_map/ppermute | solution.py:280
  337.4 9.0 %tiles.9 = (f32[2,384,128]{2,1,0:T(8,128)}, f32[2,384,128]{2,1,0:T(8,128)}) custom-call(s32[18]{0:T(128)} %select_reduce_fusion.tiles_ref, s32[1]{0:T(128)} %bitcast.4.count_ref, s32[4]{0:T(128)} %pad_add_fusion.place_ref, bf16[18,512,1024]{2,1,0:T(8,128)(2,1)} %halve.1.parts_ref, f32[4,384,128]{2,1,0:T(8,128)} %copy-done.2, f32[4,384,128]{2,1,0:T(8,128)} %copy-done.6), custom_call_target="tpu_custom_call" | custom-call | flops 3623878656 | bytes 18874368 | tf_op jit(solution)/shard_map/tiles/pallas_call | solution.py:185
  347.5 4.7 finish.8
  352.2 1.3 slice_bitcast_fusion.1
  354.3 4.3 finish.9
  363.3 22.8 %all-to-all-start.2 = ((f32[16,32,384]{2,1,0:T(8,128)}), f32[16,32,384]{2,1,0:T(8,128)S(1)}, u32[]{:S(2)}, u32[]{:S(2)}) async-start(f32[16,32,384]{2,1,0:T(8,128)} %bitcast.46), calls=%async_computation.2 | async-start | bytes 1572864 | tf_op jit(solution)/shard_map/all_to_all | solution.py:386
  387.1 8.8 %tiles.5 = (f32[2,384,128]{2,1,0:T(8,128)}, f32[2,384,128]{2,1,0:T(8,128)}) custom-call(s32[18]{0:T(128)} %select_reduce_fusion.tiles_ref, s32[1]{0:T(128)} %bitcast.4.count_ref, s32[4]{0:T(128)} %pad_add_fusion.place_ref, bf16[18,512,1024]{2,1,0:T(8,128)(2,1)} %halve.1.parts_ref, f32[4,384,128]{2,1,0:T(8,128)} %copy-done.1, f32[4,384,128]{2,1,0:T(8,128)} %copy-done.5), custom_call_target="tpu_custom_call" | custom-call | flops 3623878656 | bytes 18874368 | tf_op jit(solution)/shard_map/tiles/pallas_call | solution.py:185
  396.1 1.9 collective-permute-done.5.came_ref
  398.7 4.4 finish.5
  403.1 1.6 dynamic-slice_bitcast_fusion.4
  404.7 14.0 %collective-permute-start.7 = (f32[384,128]{1,0:T(8,128)}, f32[384,128]{1,0:T(8,128)}, u32[]{:S(2)}, u32[]{:S(2)}) collective-permute-start(f32[384,128]{1,0:T(8,128)} %dynamic-slice_bitcast_fusion.4), channel_id=1, source_target_pairs={{0,2},{2,0},{1,3},{3,1},{4,6},{6,4},{5,7},{7,5},{8,10},{10,8},{9,1... | collective-permute-start | bytes 589832 | tf_op jit(solution)/shard_map/ppermute | solution.py:280
  420.7 15.8 %all-to-all-start.3 = ((f32[16,32,384]{2,1,0:T(8,128)}), f32[16,32,384]{2,1,0:T(8,128)S(1)}, u32[]{:S(2)}, u32[]{:S(2)}) async-start(f32[16,32,384]{2,1,0:T(8,128)} %broadcast_in_dim.34), calls=%async_computation.3 | async-start | bytes 1572864 | tf_op jit(solution)/shard_map/all_to_all | solution.py:289
  436.6 2.0 collective-permute-start.21
  438.6 1.7 fusion.12
  440.6 1.8 fusion.8
  442.4 14.9 %collective-permute-done.21 = f32[384,256]{1,0:T(8,128)S(1)} collective-permute-done((f32[384,256]{1,0:T(8,128)S(1)}, f32[384,256]{1,0:T(8,128)S(1)}, u32[]{:S(2)}, u32[]{:S(2)}) %collective-permute-start.21) | collective-permute-done | bytes 393248 | tf_op jit(solution)/shard_map/ppermute | solution.py:280
  458.4 7.5 %collective-permute-done.28 = f32[384,256]{1,0:T(8,128)S(1)} collective-permute-done((f32[384,256]{1,0:T(8,128)S(1)}, f32[384,256]{1,0:T(8,128)S(1)}, u32[]{:S(2)}, u32[]{:S(2)}) %collective-permute-start.28) | collective-permute-done | bytes 393248 | tf_op jit(solution)/shard_map/ppermute | solution.py:280
  466.6 2.4 collective-permute-done.36
  470.0 3.4 fusion
  473.4 87.7 %all-reduce.2.cloned.1.call-done = f32[1024,128]{1,0:T(8,128)} async-done(((f32[1024,128]{1,0:T(8,128)}), f32[1024,128]{1,0:T(8,128)}) %all-reduce.2.cloned.1.call-update) | async-done | bytes 524304 | tf_op jit(solution)/shard_map/psum | solution.py:380
  561.1 2.1 fusion.2
  563.2 1.2 broadcast_select_fusion.3
  564.4 2.8 fusion.1
  (138 shorter events, 30.3 us)
Async XLA Ops:
  7.2 4.9 copy-start
  12.2 12.2 %collective-permute-start.11 = (f32[384,256]{1,0:T(8,128)S(1)}, f32[384,256]{1,0:T(8,128)S(1)}, u32[]{:S(2)}, u32[]{:S(2)}) collective-permute-start(f32[384,256]{1,0:T(8,128)S(1)} %get-tuple-element.66), channel_id=1, source_target_pairs={{3,0},{11,1},{19,2},{27,3},{7,4},{15,5},{23,6},{31,7},{0,8},{8,9},... | collective-permute-start | bytes 1179656 | tf_op jit(solution)/shard_map/ppermute | solution.py:348
  15.3 17.5 %collective-permute-start.10 = (f32[384,256]{1,0:T(8,128)S(1)}, f32[384,256]{1,0:T(8,128)S(1)}, u32[]{:S(2)}, u32[]{:S(2)}) collective-permute-start(f32[384,256]{1,0:T(8,128)S(1)} %get-tuple-element.66), channel_id=1, source_target_pairs={{2,0},{10,1},{18,2},{26,3},{6,4},{14,5},{22,6},{30,7},{3,8},{11,9}... | collective-permute-start | bytes 1179656 | tf_op jit(solution)/shard_map/ppermute | solution.py:348
  17.7 26.4 %collective-permute-start.9 = (f32[384,256]{1,0:T(8,128)S(1)}, f32[384,256]{1,0:T(8,128)S(1)}, u32[]{:S(2)}, u32[]{:S(2)}) collective-permute-start(f32[384,256]{1,0:T(8,128)S(1)} %get-tuple-element.66), channel_id=1, source_target_pairs={{1,0},{9,1},{17,2},{25,3},{5,4},{13,5},{21,6},{29,7},{2,8},{10,9},... | collective-permute-start | bytes 1179656 | tf_op jit(solution)/shard_map/ppermute | solution.py:348
  18.8 26.1 %collective-permute-start.8 = (f32[384,256]{1,0:T(8,128)S(1)}, f32[384,256]{1,0:T(8,128)S(1)}, u32[]{:S(2)}, u32[]{:S(2)}) collective-permute-start(f32[384,256]{1,0:T(8,128)S(1)} %get-tuple-element.66), channel_id=1, source_target_pairs={{0,0},{8,1},{16,2},{24,3},{4,4},{12,5},{20,6},{28,7},{1,8},{9,9},{... | collective-permute-start | bytes 1179656 | tf_op jit(solution)/shard_map/ppermute | solution.py:348
  20.2 26.2 %collective-permute-start.3 = (f32[384,128]{1,0:T(8,128)S(1)}, f32[384,128]{1,0:T(8,128)S(1)}, u32[]{:S(2)}, u32[]{:S(2)}) collective-permute-start(f32[384,128]{1,0:T(8,128)S(1)} %get-tuple-element.63), channel_id=1, source_target_pairs={{3,0},{11,1},{19,2},{27,3},{7,4},{15,5},{23,6},{31,7},{0,8},{8,9},... | collective-permute-start | bytes 589832 | tf_op jit(solution)/shard_map/ppermute | solution.py:348
  24.4 25.4 %collective-permute-start.2 = (f32[384,128]{1,0:T(8,128)S(1)}, f32[384,128]{1,0:T(8,128)S(1)}, u32[]{:S(2)}, u32[]{:S(2)}) collective-permute-start(f32[384,128]{1,0:T(8,128)S(1)} %get-tuple-element.63), channel_id=1, source_target_pairs={{2,0},{10,1},{18,2},{26,3},{6,4},{14,5},{22,6},{30,7},{3,8},{11,9}... | collective-permute-start | bytes 589832 | tf_op jit(solution)/shard_map/ppermute | solution.py:348
  32.8 19.4 %collective-permute-start.1 = (f32[384,128]{1,0:T(8,128)S(1)}, f32[384,128]{1,0:T(8,128)S(1)}, u32[]{:S(2)}, u32[]{:S(2)}) collective-permute-start(f32[384,128]{1,0:T(8,128)S(1)} %get-tuple-element.63), channel_id=1, source_target_pairs={{1,0},{9,1},{17,2},{25,3},{5,4},{13,5},{21,6},{29,7},{2,8},{10,9},... | collective-permute-start | bytes 589832 | tf_op jit(solution)/shard_map/ppermute | solution.py:348
  44.2 8.1 %collective-permute-start = (f32[384,128]{1,0:T(8,128)S(1)}, f32[384,128]{1,0:T(8,128)S(1)}, u32[]{:S(2)}, u32[]{:S(2)}) collective-permute-start(f32[384,128]{1,0:T(8,128)S(1)} %get-tuple-element.63), channel_id=1, source_target_pairs={{0,0},{8,1},{16,2},{24,3},{4,4},{12,5},{20,6},{28,7},{1,8},{9,9},{... | collective-permute-start | bytes 589832 | tf_op jit(solution)/shard_map/ppermute | solution.py:348
  45.0 58.3 %copy-start.3 = (f32[4,384,256]{2,1,0:T(8,128)}, f32[4,384,256]{2,1,0:T(8,128)S(1)}, u32[]{:S(2)}) copy-start(f32[4,384,256]{2,1,0:T(8,128)S(1)} %pad_maximum_fusion.refs_0_) | copy-start | bytes 4718596
  45.0 90.4 %collective-permute-start.12 = (f32[4,384,256]{2,1,0:T(8,128)S(1)}, f32[4,384,256]{2,1,0:T(8,128)}, u32[]{:S(2)}, u32[]{:S(2)}) collective-permute-start(f32[4,384,256]{2,1,0:T(8,128)S(1)} %pad_maximum_fusion.refs_0_), channel_id=1, source_target_pairs={{0,4},{4,0},{1,5},{5,1},{2,6},{6,2},{3,7},{7,3},{8,12},{12,8},{9,1... | collective-permute-start | bytes 4718600 | tf_op jit(solution)/shard_map/ppermute | solution.py:280
  46.4 56.9 %copy-start.19 = (f32[384,128]{1,0:T(8,128)}, f32[384,128]{1,0:T(8,128)S(1)}, u32[]{:S(2)}) copy-start(f32[384,128]{1,0:T(8,128)S(1)} %collective-permute-done.3) | copy-start | bytes 589828
  49.7 53.5 %copy-start.21 = (f32[384,128]{1,0:T(8,128)}, f32[384,128]{1,0:T(8,128)S(1)}, u32[]{:S(2)}) copy-start(f32[384,128]{1,0:T(8,128)S(1)} %collective-permute-done.2) | copy-start | bytes 589828
  52.3 51.0 %copy-start.23 = (f32[384,128]{1,0:T(8,128)}, f32[384,128]{1,0:T(8,128)S(1)}, u32[]{:S(2)}) copy-start(f32[384,128]{1,0:T(8,128)S(1)} %collective-permute-done.1) | copy-start | bytes 589828
  52.3 51.0 %copy-start.25 = (f32[384,128]{1,0:T(8,128)}, f32[384,128]{1,0:T(8,128)S(1)}, u32[]{:S(2)}) copy-start(f32[384,128]{1,0:T(8,128)S(1)} %collective-permute-done) | copy-start | bytes 589828
  52.3 36.6 %collective-permute-start.18 = (f32[384,256]{1,0:T(8,128)S(1)}, f32[384,256]{1,0:T(8,128)S(1)}, u32[]{:S(2)}, u32[]{:S(2)}) collective-permute-start(f32[384,256]{1,0:T(8,128)S(1)} %get-tuple-element.35), channel_id=1, source_target_pairs={{3,0},{11,1},{19,2},{27,3},{7,4},{15,5},{23,6},{31,7},{0,8},{8,9},... | collective-permute-start | bytes 1179656 | tf_op jit(solution)/shard_map/ppermute | solution.py:348
  68.1 28.0 %collective-permute-start.17 = (f32[384,256]{1,0:T(8,128)S(1)}, f32[384,256]{1,0:T(8,128)S(1)}, u32[]{:S(2)}, u32[]{:S(2)}) collective-permute-start(f32[384,256]{1,0:T(8,128)S(1)} %get-tuple-element.35), channel_id=1, source_target_pairs={{2,0},{10,1},{18,2},{26,3},{6,4},{14,5},{22,6},{30,7},{3,8},{11,9}... | collective-permute-start | bytes 1179656 | tf_op jit(solution)/shard_map/ppermute | solution.py:348
  88.2 13.8 %collective-permute-start.16 = (f32[384,256]{1,0:T(8,128)S(1)}, f32[384,256]{1,0:T(8,128)S(1)}, u32[]{:S(2)}, u32[]{:S(2)}) collective-permute-start(f32[384,256]{1,0:T(8,128)S(1)} %get-tuple-element.35), channel_id=1, source_target_pairs={{1,0},{9,1},{17,2},{25,3},{5,4},{13,5},{21,6},{29,7},{2,8},{10,9},... | collective-permute-start | bytes 1179656 | tf_op jit(solution)/shard_map/ppermute | solution.py:348
  88.2 13.8 %collective-permute-start.15 = (f32[384,256]{1,0:T(8,128)S(1)}, f32[384,256]{1,0:T(8,128)S(1)}, u32[]{:S(2)}, u32[]{:S(2)}) collective-permute-start(f32[384,256]{1,0:T(8,128)S(1)} %get-tuple-element.35), channel_id=1, source_target_pairs={{0,0},{8,1},{16,2},{24,3},{4,4},{12,5},{20,6},{28,7},{1,8},{9,9},{... | collective-permute-start | bytes 1179656 | tf_op jit(solution)/shard_map/ppermute | solution.py:348
  103.3 43.1 %collective-permute-start.19 = (f32[4,384,256]{2,1,0:T(8,128)}, f32[4,384,256]{2,1,0:T(8,128)}, u32[]{:S(2)}, u32[]{:S(2)}) collective-permute-start(f32[4,384,256]{2,1,0:T(8,128)} %pad_maximum_fusion.1.refs_0_), channel_id=1, source_target_pairs={{0,4},{4,0},{1,5},{5,1},{2,6},{6,2},{3,7},{7,3},{8,12},{12,8},{9,1... | collective-permute-start | bytes 4718600 | tf_op jit(solution)/shard_map/ppermute | solution.py:280
  104.8 52.6 %collective-permute-start.6 = (f32[384,1024]{1,0:T(8,128)S(1)}, f32[384,1024]{1,0:T(8,128)}, u32[]{:S(2)}, u32[]{:S(2)}) collective-permute-start(f32[384,1024]{1,0:T(8,128)S(1)} %copy-done), channel_id=1, source_target_pairs={{0,2},{2,0},{1,3},{3,1},{4,6},{6,4},{5,7},{7,5},{8,10},{10,8},{9,1... | collective-permute-start | bytes 4718600 | tf_op jit(solution)/shard_map/ppermute | solution.py:280
  146.3 15.6 %collective-permute-start.13 = (f32[2,384,256]{2,1,0:T(8,128)}, f32[2,384,256]{2,1,0:T(8,128)S(1)}, u32[]{:S(2)}, u32[]{:S(2)}) collective-permute-start(f32[2,384,256]{2,1,0:T(8,128)} %get-tuple-element.33), channel_id=1, source_target_pairs={{0,1},{1,0},{2,3},{3,2},{4,5},{5,4},{6,7},{7,6},{8,9},{9,8},{10,11... | collective-permute-start | bytes 2359304 | tf_op jit(solution)/shard_map/ppermute | solution.py:280
  157.4 11.4 %collective-permute-start.20 = (f32[2,384,256]{2,1,0:T(8,128)}, f32[2,384,256]{2,1,0:T(8,128)S(1)}, u32[]{:S(2)}, u32[]{:S(2)}) collective-permute-start(f32[2,384,256]{2,1,0:T(8,128)} %get-tuple-element.37), channel_id=1, source_target_pairs={{0,1},{1,0},{2,3},{3,2},{4,5},{5,4},{6,7},{7,6},{8,9},{9,8},{10,11... | collective-permute-start | bytes 2359304 | tf_op jit(solution)/shard_map/ppermute | solution.py:280
  175.9 39.9 %collective-permute-start.29 = (f32[512,512]{1,0:T(8,128)S(1)}, f32[512,512]{1,0:T(8,128)S(1)}, u32[]{:S(2)}, u32[]{:S(2)}) collective-permute-start(f32[512,512]{1,0:T(8,128)S(1)} %pad_maximum_fusion.3), channel_id=1, source_target_pairs={{0,1},{1,0},{2,3},{3,2},{4,5},{5,4},{6,7},{7,6},{8,9},{9,8},{10,11... | collective-permute-start | bytes 3145736 | tf_op jit(solution)/shard_map/ppermute | solution.py:280
  176.4 17.9 %collective-permute-start.25 = (f32[384,256]{1,0:T(8,128)S(1)}, f32[384,256]{1,0:T(8,128)S(1)}, u32[]{:S(2)}, u32[]{:S(2)}) collective-permute-start(f32[384,256]{1,0:T(8,128)S(1)} %get-tuple-element.39), channel_id=1, source_target_pairs={{3,0},{11,1},{19,2},{27,3},{7,4},{15,5},{23,6},{31,7},{0,8},{8,9},... | collective-permute-start | bytes 1179656 | tf_op jit(solution)/shard_map/ppermute | solution.py:348
  176.4 26.8 %collective-permute-start.24 = (f32[384,256]{1,0:T(8,128)S(1)}, f32[384,256]{1,0:T(8,128)S(1)}, u32[]{:S(2)}, u32[]{:S(2)}) collective-permute-start(f32[384,256]{1,0:T(8,128)S(1)} %get-tuple-element.39), channel_id=1, source_target_pairs={{2,0},{10,1},{18,2},{26,3},{6,4},{14,5},{22,6},{30,7},{3,8},{11,9}... | collective-permute-start | bytes 1179656 | tf_op jit(solution)/shard_map/ppermute | solution.py:348
  193.7 18.0 %collective-permute-start.23 = (f32[384,256]{1,0:T(8,128)S(1)}, f32[384,256]{1,0:T(8,128)S(1)}, u32[]{:S(2)}, u32[]{:S(2)}) collective-permute-start(f32[384,256]{1,0:T(8,128)S(1)} %get-tuple-element.39), channel_id=1, source_target_pairs={{1,0},{9,1},{17,2},{25,3},{5,4},{13,5},{21,6},{29,7},{2,8},{10,9},... | collective-permute-start | bytes 1179656 | tf_op jit(solution)/shard_map/ppermute | solution.py:348
  193.7 18.0 %collective-permute-start.22 = (f32[384,256]{1,0:T(8,128)S(1)}, f32[384,256]{1,0:T(8,128)S(1)}, u32[]{:S(2)}, u32[]{:S(2)}) collective-permute-start(f32[384,256]{1,0:T(8,128)S(1)} %get-tuple-element.39), channel_id=1, source_target_pairs={{0,0},{8,1},{16,2},{24,3},{4,4},{12,5},{20,6},{28,7},{1,8},{9,9},{... | collective-permute-start | bytes 1179656 | tf_op jit(solution)/shard_map/ppermute | solution.py:348
  211.8 5.2 copy-start.4
  211.8 43.7 %collective-permute-start.26 = (f32[4,384,256]{2,1,0:T(8,128)S(1)}, f32[4,384,256]{2,1,0:T(8,128)}, u32[]{:S(2)}, u32[]{:S(2)}) collective-permute-start(f32[4,384,256]{2,1,0:T(8,128)S(1)} %pad_maximum_fusion.2.refs_0_), channel_id=1, source_target_pairs={{0,4},{4,0},{1,5},{5,1},{2,6},{6,2},{3,7},{7,3},{8,12},{12,8},{9,1... | collective-permute-start | bytes 4718600 | tf_op jit(solution)/shard_map/ppermute | solution.py:280
  217.0 51.3 %all-to-all-start = ((f32[16,32,512]{2,1,0:T(8,128)}), f32[16,32,512]{2,1,0:T(8,128)S(1)}, u32[]{:S(2)}, u32[]{:S(2)}) async-start(f32[16,32,512]{2,1,0:T(8,128)} %bitcast.33), calls=%async_computation | async-start | bytes 2097152 | tf_op jit(solution)/shard_map/all_to_all | solution.py:386
  268.3 27.2 %copy-start.27 = (f32[384,128]{1,0:T(8,128)S(1)}, f32[384,128]{1,0:T(8,128)}, u32[]{:S(2)}) copy-start(f32[384,128]{1,0:T(8,128)} %get-tuple-element.47) | copy-start | bytes 589828
  269.5 84.0 %all-to-all-start.1 = ((f32[16,32,512]{2,1,0:T(8,128)}), f32[16,32,512]{2,1,0:T(8,128)S(1)}, u32[]{:S(2)}, u32[]{:S(2)}) async-start(f32[16,32,512]{2,1,0:T(8,128)} %broadcast_in_dim.33), calls=%async_computation.1 | async-start | bytes 2097152 | tf_op jit(solution)/shard_map/all_to_all | solution.py:289
  295.6 21.3 %collective-permute-start.33 = (f32[384,128]{1,0:T(8,128)S(1)}, f32[384,128]{1,0:T(8,128)S(1)}, u32[]{:S(2)}, u32[]{:S(2)}) collective-permute-start(f32[384,128]{1,0:T(8,128)S(1)} %copy-done.27), channel_id=1, source_target_pairs={{3,0},{11,1},{19,2},{27,3},{7,4},{15,5},{23,6},{31,7},{0,8},{8,9},... | collective-permute-start | bytes 589832 | tf_op jit(solution)/shard_map/ppermute | solution.py:348
  297.6 21.5 %collective-permute-start.32 = (f32[384,128]{1,0:T(8,128)S(1)}, f32[384,128]{1,0:T(8,128)S(1)}, u32[]{:S(2)}, u32[]{:S(2)}) collective-permute-start(f32[384,128]{1,0:T(8,128)S(1)} %copy-done.27), channel_id=1, source_target_pairs={{2,0},{10,1},{18,2},{26,3},{6,4},{14,5},{22,6},{30,7},{3,8},{11,9}... | collective-permute-start | bytes 589832 | tf_op jit(solution)/shard_map/ppermute | solution.py:348
  299.9 21.2 %collective-permute-start.31 = (f32[384,128]{1,0:T(8,128)S(1)}, f32[384,128]{1,0:T(8,128)S(1)}, u32[]{:S(2)}, u32[]{:S(2)}) collective-permute-start(f32[384,128]{1,0:T(8,128)S(1)} %copy-done.27), channel_id=1, source_target_pairs={{1,0},{9,1},{17,2},{25,3},{5,4},{13,5},{21,6},{29,7},{2,8},{10,9},... | collective-permute-start | bytes 589832 | tf_op jit(solution)/shard_map/ppermute | solution.py:348
  301.1 20.1 %collective-permute-start.30 = (f32[384,128]{1,0:T(8,128)S(1)}, f32[384,128]{1,0:T(8,128)S(1)}, u32[]{:S(2)}, u32[]{:S(2)}) collective-permute-start(f32[384,128]{1,0:T(8,128)S(1)} %copy-done.27), channel_id=1, source_target_pairs={{0,0},{8,1},{16,2},{24,3},{4,4},{12,5},{20,6},{28,7},{1,8},{9,9},{... | collective-permute-start | bytes 589832 | tf_op jit(solution)/shard_map/ppermute | solution.py:348
  321.2 15.3 %copy-start.2 = (f32[4,384,128]{2,1,0:T(8,128)}, f32[4,384,128]{2,1,0:T(8,128)S(1)}, u32[]{:S(2)}) copy-start(f32[4,384,128]{2,1,0:T(8,128)S(1)} %pad_maximum_fusion.5.refs_0_) | copy-start | bytes 2359300
  321.2 15.3 %collective-permute-start.34 = (f32[4,384,128]{2,1,0:T(8,128)S(1)}, f32[4,384,128]{2,1,0:T(8,128)S(1)}, u32[]{:S(2)}, u32[]{:S(2)}) collective-permute-start(f32[4,384,128]{2,1,0:T(8,128)S(1)} %pad_maximum_fusion.5.refs_0_), channel_id=1, source_target_pairs={{0,4},{4,0},{1,5},{5,1},{2,6},{6,2},{3,7},{7,3},{8,12},{12,8},{9,1... | collective-permute-start | bytes 2359304 | tf_op jit(solution)/shard_map/ppermute | solution.py:280
  323.0 23.5 %collective-permute-start.27 = (f32[2,384,256]{2,1,0:T(8,128)}, f32[2,384,256]{2,1,0:T(8,128)S(1)}, u32[]{:S(2)}, u32[]{:S(2)}) collective-permute-start(f32[2,384,256]{2,1,0:T(8,128)} %get-tuple-element.41), channel_id=1, source_target_pairs={{0,1},{1,0},{2,3},{3,2},{4,5},{5,4},{6,7},{7,6},{8,9},{9,8},{10,11... | collective-permute-start | bytes 2359304 | tf_op jit(solution)/shard_map/ppermute | solution.py:280
  346.5 7.0 %collective-permute-start.35 = (f32[2,384,128]{2,1,0:T(8,128)}, f32[2,384,128]{2,1,0:T(8,128)S(1)}, u32[]{:S(2)}, u32[]{:S(2)}) collective-permute-start(f32[2,384,128]{2,1,0:T(8,128)} %get-tuple-element.51), channel_id=1, source_target_pairs={{0,1},{1,0},{2,3},{3,2},{4,5},{5,4},{6,7},{7,6},{8,9},{9,8},{10,11... | collective-permute-start | bytes 1179656 | tf_op jit(solution)/shard_map/ppermute | solution.py:280
  358.6 1.8 copy-start.22
  358.6 1.8 copy-start.24
  359.8 2.5 collective-permute-start.38
  360.5 2.8 copy-start.1
  360.5 25.7 %collective-permute-start.4 = (f32[4,384,128]{2,1,0:T(8,128)S(1)}, f32[4,384,128]{2,1,0:T(8,128)S(1)}, u32[]{:S(2)}, u32[]{:S(2)}) collective-permute-start(f32[4,384,128]{2,1,0:T(8,128)S(1)} %pad_maximum_fusion.4.refs_0_), channel_id=1, source_target_pairs={{0,4},{4,0},{1,5},{5,1},{2,6},{6,2},{3,7},{7,3},{8,12},{12,8},{9,1... | collective-permute-start | bytes 2359304 | tf_op jit(solution)/shard_map/ppermute | solution.py:280
  363.3 56.3 %all-to-all-start.2 = ((f32[16,32,384]{2,1,0:T(8,128)}), f32[16,32,384]{2,1,0:T(8,128)S(1)}, u32[]{:S(2)}, u32[]{:S(2)}) async-start(f32[16,32,384]{2,1,0:T(8,128)} %bitcast.46), calls=%async_computation.2 | async-start | bytes 1572864 | tf_op jit(solution)/shard_map/all_to_all | solution.py:386
  386.2 175.0 %all-reduce.2.cloned.1.call-start = ((), (), s32[]{:S(2)}) async-start(), calls=%async_computation.4 | async-start | bytes 1048576 | tf_op jit(solution)/shard_map/psum | solution.py:380
  396.0 2.0 collective-permute-start.5
  398.7 20.0 %copy-start.10 = (f32[2,384,256]{2,1,0:T(8,128)S(1)}, f32[2,384,256]{2,1,0:T(8,128)}, u32[]{:S(2)}) copy-start(f32[2,384,256]{2,1,0:T(8,128)} %get-tuple-element.34) | copy-start | bytes 2359300
  404.7 33.8 %collective-permute-start.7 = (f32[384,128]{1,0:T(8,128)}, f32[384,128]{1,0:T(8,128)}, u32[]{:S(2)}, u32[]{:S(2)}) collective-permute-start(f32[384,128]{1,0:T(8,128)} %dynamic-slice_bitcast_fusion.4), channel_id=1, source_target_pairs={{0,2},{2,0},{1,3},{3,1},{4,6},{6,4},{5,7},{7,5},{8,10},{10,8},{9,1... | collective-permute-start | bytes 589832 | tf_op jit(solution)/shard_map/ppermute | solution.py:280
  419.6 16.9 %copy-start.12 = (f32[2,384,256]{2,1,0:T(8,128)S(1)}, f32[2,384,256]{2,1,0:T(8,128)}, u32[]{:S(2)}) copy-start(f32[2,384,256]{2,1,0:T(8,128)} %get-tuple-element.38) | copy-start | bytes 2359300
  419.6 21.0 %collective-permute-start.14 = (f32[384,256]{1,0:T(8,128)}, f32[384,256]{1,0:T(8,128)}, u32[]{:S(2)}, u32[]{:S(2)}) collective-permute-start(f32[384,256]{1,0:T(8,128)} %dynamic-slice_bitcast_fusion.2), channel_id=1, source_target_pairs={{0,2},{2,0},{1,3},{3,1},{4,6},{6,4},{5,7},{7,5},{8,10},{10,8},{9,1... | collective-permute-start | bytes 1179656 | tf_op jit(solution)/shard_map/ppermute | solution.py:280
  420.7 19.6 %copy-start.14 = (f32[2,384,256]{2,1,0:T(8,128)S(1)}, f32[2,384,256]{2,1,0:T(8,128)}, u32[]{:S(2)}) copy-start(f32[2,384,256]{2,1,0:T(8,128)} %get-tuple-element.42) | copy-start | bytes 2359300
  420.7 49.0 %all-to-all-start.3 = ((f32[16,32,384]{2,1,0:T(8,128)}), f32[16,32,384]{2,1,0:T(8,128)S(1)}, u32[]{:S(2)}, u32[]{:S(2)}) async-start(f32[16,32,384]{2,1,0:T(8,128)} %broadcast_in_dim.34), calls=%async_computation.3 | async-start | bytes 1572864 | tf_op jit(solution)/shard_map/all_to_all | solution.py:289
  436.5 4.1 copy-start.11
  436.5 20.8 %copy-start.13 = (f32[2,384,256]{2,1,0:T(8,128)S(1)}, f32[2,384,256]{2,1,0:T(8,128)}, u32[]{:S(2)}) copy-start(f32[2,384,256]{2,1,0:T(8,128)} %get-tuple-element.38) | copy-start | bytes 2359300
  436.6 20.7 %collective-permute-start.21 = (f32[384,256]{1,0:T(8,128)S(1)}, f32[384,256]{1,0:T(8,128)S(1)}, u32[]{:S(2)}, u32[]{:S(2)}) collective-permute-start(f32[384,256]{1,0:T(8,128)S(1)} %dynamic-slice_bitcast_fusion.1), channel_id=1, source_target_pairs={{0,2},{2,0},{1,3},{3,1},{4,6},{6,4},{5,7},{7,5},{8,10},{10,8},{9,1... | collective-permute-start | bytes 1179656 | tf_op jit(solution)/shard_map/ppermute | solution.py:280
  440.3 17.8 %copy-start.18 = (f32[2,384,128]{2,1,0:T(8,128)S(1)}, f32[2,384,128]{2,1,0:T(8,128)}, u32[]{:S(2)}) copy-start(f32[2,384,128]{2,1,0:T(8,128)} %get-tuple-element.52) | copy-start | bytes 1179652
  440.3 25.5 %copy-start.15 = (f32[2,384,256]{2,1,0:T(8,128)S(1)}, f32[2,384,256]{2,1,0:T(8,128)}, u32[]{:S(2)}) copy-start(f32[2,384,256]{2,1,0:T(8,128)} %get-tuple-element.42) | copy-start | bytes 2359300
  440.3 25.5 %collective-permute-start.28 = (f32[384,256]{1,0:T(8,128)S(1)}, f32[384,256]{1,0:T(8,128)S(1)}, u32[]{:S(2)}, u32[]{:S(2)}) collective-permute-start(f32[384,256]{1,0:T(8,128)S(1)} %dynamic-slice_bitcast_fusion), channel_id=1, source_target_pairs={{0,2},{2,0},{1,3},{3,1},{4,6},{6,4},{5,7},{7,5},{8,10},{10,8},{9,1... | collective-permute-start | bytes 1179656 | tf_op jit(solution)/shard_map/ppermute | solution.py:280
  440.6 29.1 %collective-permute-start.37 = (f32[512,512]{1,0:T(8,128)S(1)}, f32[512,512]{1,0:T(8,128)S(1)}, u32[]{:S(2)}, u32[]{:S(2)}) collective-permute-start(f32[512,512]{1,0:T(8,128)S(1)} %bitcast.90), channel_id=1, source_target_pairs={{0,1},{1,0},{2,3},{3,2},{4,5},{5,4},{6,7},{7,6},{8,9},{9,8},{10,11... | collective-permute-start | bytes 3145736 | tf_op jit(solution)/shard_map/ppermute | solution.py:280
  458.1 10.9 %collective-permute-start.36 = (f32[384,128]{1,0:T(8,128)S(1)}, f32[384,128]{1,0:T(8,128)S(1)}, u32[]{:S(2)}, u32[]{:S(2)}) collective-permute-start(f32[384,128]{1,0:T(8,128)S(1)} %dynamic-slice_bitcast_fusion.3), channel_id=1, source_target_pairs={{0,2},{2,0},{1,3},{3,1},{4,6},{6,4},{5,7},{7,5},{8,10},{10,8},{9,1... | collective-permute-start | bytes 589832 | tf_op jit(solution)/shard_map/ppermute | solution.py:280
  469.7 93.5 %collective-permute-start.39 = (f32[512,384]{1,0:T(8,128)S(1)}, f32[512,384]{1,0:T(8,128)}, u32[]{:S(2)}, u32[]{:S(2)}) collective-permute-start(f32[512,384]{1,0:T(8,128)S(1)} %bitcast.91), channel_id=1, source_target_pairs={{0,1},{1,0},{2,3},{3,2},{4,5},{5,4},{6,7},{7,6},{8,9},{9,8},{10,11... | collective-permute-start | bytes 2359304 | tf_op jit(solution)/shard_map/ppermute | solution.py:280
  (9 other events, 9.6 us)
Sparse Core Ops, SparseCore 0:
  418.9 142.2 all-reduce.1
